TPU v7x, 32 devices: a whole 2x2x4 slice. The times are simulated.
32 devices in a mesh: sub: 8 (over z, x), blk: 4 (over y, core).
Axes of the slice: x: 2, y: 2, z: 4, core: 2. Of those that a mesh axis runs over, the one named last changes fastest.
Arguments:
- coefficients: float32 [512, 4, 2, 64, 128], P('sub', None, None, 'blk'), may hold values from -0.2 to 0.2
- owner_slot: int32 [512], P('sub'), may hold values from 0 to 511, as said below
- child_list: int32 [512, 8], P('sub'), may hold values from 0 to 7, each once within a row
Outputs:
- children: float32 [512, 4, 8, 64, 2, 128], P('sub', None, None, 'blk')
Inputs may be any that keep to these rules, and one draw needn't show every extreme that they name: owner_slot is a permutation of the 512 positions; position s belongs to subtree index s // 64; of the 64 boxes held by one subtree index exactly 8 belong to each subtree index. `child_list`: each row lists the 8 octant codes once each.
All inputs are finite; a program needn't handle non-finite values.
Results may differ from a plain program's by a relative error of at most 0.0003.
Values sent between devices are 32-bit elements; how exact they have to be, the bound alone decides.
A program may use at most 128 MiB of HBM per device.

v0:
```python
import functools
import math

import jax
import jax.numpy as jnp
import numpy as np
from jax import lax
from jax.experimental import pallas as pl
from jax.experimental.pallas import tpu as pltpu
from jax.sharding import PartitionSpec as P

J = 64
K = 128
GROUP = 4


def legendre_constants(degrees, columns):
    q = np.abs(np.arange(columns) - degrees).astype(np.float64)
    log_norm = np.array(
        [
            0.5
            * (
                math.log((2 * v + 1) / (4 * math.pi))
                + math.lgamma(2 * v + 1)
                - v * math.log(4.0)
                - 2 * math.lgamma(v + 1)
            )
            for v in q
        ]
    )
    l = np.arange(degrees, dtype=np.float64)[:, None]
    numer = np.maximum(4 * l * l - 1, 1.0)
    denom = np.maximum(l * l - q[None] ** 2, 1.0)
    factor = np.sqrt(numer / denom)
    before = np.ones_like(factor)
    before[1:] = 1.0 / factor[:-1]
    return (
        log_norm.astype(np.float32)[None],
        q.astype(np.float32)[None],
        factor.astype(np.float32)[:, None, :],
        before.astype(np.float32)[:, None, :],
    )


def wave_matrix(degrees, columns, azimuths):
    turns = ((np.arange(columns)[:, None] - degrees) * np.arange(azimuths)[None, :]) % azimuths
    angle = 2.0 * np.pi * turns / azimuths
    cosine, sine = np.cos(angle), np.sin(angle)
    left = np.concatenate([cosine, -sine], axis=0)
    right = np.concatenate([-sine, -cosine], axis=0)
    return np.concatenate([left, right], axis=1).astype(np.float32)


def phase_tables(polar, azimuths):
    azimuth = 2.0 * jnp.pi * jnp.arange(azimuths).astype(jnp.float32) / azimuths
    octants = jnp.arange(8, dtype=jnp.int32)
    dir_x = jnp.sin(polar)[:, None] * jnp.cos(azimuth)[None, :]
    dir_y = jnp.sin(polar)[:, None] * jnp.sin(azimuth)[None, :]
    dir_z = jnp.cos(polar)[:, None] * jnp.ones_like(azimuth)[None, :]
    sign_x = (2 * (octants & 1) - 1).astype(jnp.float32)[:, None, None]
    sign_y = (2 * (octants >> 1 & 1) - 1).astype(jnp.float32)[:, None, None]
    sign_z = (2 * (octants >> 2 & 1) - 1).astype(jnp.float32)[:, None, None]
    phase = 5.5 * (sign_x * dir_x[None] + sign_y * dir_y[None] + sign_z * dir_z[None])
    return jnp.repeat(jnp.cos(phase), 2, axis=1), jnp.repeat(jnp.sin(phase), 2, axis=1)


def fill_table(tab, diag_ref, cos_ref, order_ref, factor_ref, before_ref):
    degrees = tab.shape[0]
    diag = diag_ref[...]
    cosines = cos_ref[...]
    order = jnp.broadcast_to(order_ref[...], diag.shape)
    next_value = jnp.sqrt(2.0 * order + 3.0) * cosines * diag

    def advance(degree, state):
        previous, before = state
        level = lax.convert_element_type(degree, jnp.float32)
        recur = factor_ref[degree] * (cosines * previous - before * before_ref[degree])
        value = jnp.where(level == order + 1.0, next_value, recur)
        value = jnp.where(level == order, diag, value)
        value = jnp.where(level < order, 0.0, value)
        tab[degree] = value
        return value, previous

    zeros = diag - diag
    lax.fori_loop(0, degrees, advance, (zeros, zeros))


def transform(source, child, *refs):
    cycles = refs[:GROUP]
    matrix, phase_cos, phase_sin, out, upper, lower = refs[GROUP:]
    step = pl.program_id(0)
    _, lines, width, _ = cycles[0].shape
    cases = lines // 2
    rows = 2 * width
    for box in range(GROUP):
        for case in range(cases):
            base = (box * cases + case) * rows
            real, imag = cycles[box][0, 2 * case], cycles[box][0, 2 * case + 1]
            upper[pl.ds(base, width, 2), :] = real
            upper[pl.ds(base + 1, width, 2), :] = imag
            lower[pl.ds(base, width, 2), :] = imag
            lower[pl.ds(base + 1, width, 2), :] = -real
    both = jnp.concatenate([upper[...], lower[...]], axis=1)
    spread = jnp.dot(both, matrix[...], precision=lax.Precision.HIGHEST, preferred_element_type=jnp.float32)
    for box in range(GROUP):
        for place in range(8):
            octant = child[(step * GROUP + box) * 8 + place]
            turn_cos = phase_cos[octant]
            turn_sin = phase_sin[octant]
            for case in range(cases):
                base = (box * cases + case) * rows
                wave = spread[base : base + rows, :K]
                quarter = spread[base : base + rows, K:]
                out[box, case, place] = wave * turn_cos + quarter * turn_sin


def own_polar(parts, blk_index):
    width = J // parts
    polar_all = jnp.pi * (jnp.arange(J).astype(jnp.float32) + 0.5) / J
    return lax.dynamic_slice_in_dim(polar_all, blk_index * width, width, 0)


def make_children(cycles, source, child_list, parts, lines, blk_index):
    boxes, _, width, columns = cycles.shape
    cases = lines // 2
    phase_cos, phase_sin = phase_tables(own_polar(parts, blk_index), K)
    matrix = jnp.asarray(wave_matrix(columns // 2, columns, K))

    def pick(offset):
        return pl.BlockSpec(
            (1, lines, width, columns),
            lambda i, source, child: (source[i * GROUP + offset], 0, 0, 0),
        )

    whole = pl.BlockSpec(memory_space=pltpu.VMEM)
    rows = GROUP * cases * 2 * width
    out = pl.pallas_call(
        transform,
        grid_spec=pltpu.PrefetchScalarGridSpec(
            num_scalar_prefetch=2,
            grid=(boxes // GROUP,),
            in_specs=[pick(n) for n in range(GROUP)] + [whole] * 3,
            out_specs=pl.BlockSpec(
                (GROUP, cases, 8, 2 * width, K), lambda i, source, child: (i, 0, 0, 0, 0)
            ),
            scratch_shapes=[
                pltpu.VMEM((rows, columns), jnp.float32),
                pltpu.VMEM((rows, columns), jnp.float32),
            ],
        ),
        out_shape=jax.ShapeDtypeStruct((boxes, cases, 8, 2 * width, K), jnp.float32),
        compiler_params=pltpu.CompilerParams(vmem_limit_bytes=40 * 1024 * 1024),
        name="transform",
    )(source, child_list.reshape(-1), *([cycles] * GROUP), matrix, phase_cos, phase_sin)
    return out.reshape(boxes, cases, 8, width, 2, K)


def swapped(index, step, size):
    total = 0
    bit = 1
    while bit < size:
        total = total + ((index // bit + step // bit) % 2) * bit
        bit *= 2
    return total


def exchange(
    sub_count,
    chips,
    blocks,
    slots,
    diag,
    cosines,
    orders,
    factor,
    before,
    cycles,
    placed,
    gathered,
    tab,
    send_far,
    recv_far,
    send_near,
    recv_near,
    send_pair,
    recv_pair,
    send_slot,
    recv_slot,
    local,
):
    per_peer = blocks.shape[1]
    steps = sub_count * per_peer
    sub = lax.axis_index("sub")
    blk = lax.axis_index("blk")
    chip = blk // 2
    core = blk % 2
    sibling = chip * 2 + (1 - core)

    def remote(source, target, send, recv, device):
        return pltpu.make_async_remote_copy(
            src_ref=source,
            dst_ref=target,
            send_sem=send,
            recv_sem=recv,
            device_id=device,
            device_id_type=pl.DeviceIdType.MESH,
        )

    def far(step, box):
        peer = swapped(sub, step, sub_count)
        return remote(
            blocks.at[peer, box],
            gathered.at[blk, sub, box],
            send_far.at[step, box],
            recv_far.at[step, box],
            (peer, blk),
        )

    def slot_copy(step):
        peer = swapped(sub, step, sub_count)
        return remote(slots.at[peer], placed.at[sub], send_slot.at[step], recv_slot.at[step], (peer, blk))

    def held(hop):
        return ((chip + chips - hop) % chips) * 2 + core

    def near(hop, step, box, own):
        source = swapped(sub, step, sub_count)
        origin = blocks.at[sub, box] if own else gathered.at[blk, source, box]
        return remote(
            origin,
            gathered.at[blk, source, box],
            send_near.at[hop - 1, step, box],
            recv_near.at[hop - 1, step, box],
            (sub, ((chip + hop) % chips) * 2 + core),
        )

    def pair(hop, step, box, own=False):
        source = swapped(sub, step, sub_count)
        part = held(hop)
        origin = blocks.at[sub, box] if own else gathered.at[part, source, box]
        return remote(
            origin,
            gathered.at[part, source, box],
            send_pair.at[hop, step, box],
            recv_pair.at[hop, step, box],
            (sub, sibling),
        )

    barrier = pltpu.get_barrier_semaphore()

    def greet(device):
        pl.semaphore_signal(barrier, inc=1, device_id=device, device_id_type=pl.DeviceIdType.MESH)

    for step in range(1, sub_count):
        greet((swapped(sub, step, sub_count), blk))
    for hop in range(1, chips):
        greet((sub, ((chip + hop) % chips) * 2 + core))
    greet((sub, sibling))
    pl.semaphore_wait(barrier, sub_count - 1 + chips)

    def relay(step, box):
        for hop in range(1, chips):
            near(hop, step, box, False).wait_recv()
            pair(hop, step, box).start()

    def arrive(step, box):
        if step > 0:
            far(step, box).wait_recv()
        for hop in range(1, chips):
            near(hop, step, box, step == 0).start()
        pair(0, step, box, step == 0).start()

    order = list(range(sub_count // 2, sub_count)) + list(range(2, sub_count // 2))
    everyone = [1] + order
    for step in everyone:
        slot_copy(step).start()

    @pl.loop(0, per_peer)
    def _(box):
        arrive(0, box)
        far(1, box).start()

        @pl.when(box < 2)
        def _():
            for step in order:
                far(step, box).start()

    keep_slot = pltpu.make_async_copy(slots.at[sub], placed.at[sub], local.at[0])
    keep_slot.start()
    keep_blocks = pltpu.make_async_copy(blocks.at[sub], gathered.at[blk, sub], local.at[1])
    keep_blocks.start()
    fill_table(tab, diag, cosines, orders, factor, before)

    parts, _, _, rows, columns = gathered.shape
    degrees, width, _ = tab.shape
    depth = degrees // parts
    lines = rows // depth

    def finish(step, box):
        source = swapped(sub, step, sub_count)
        for hop in range(chips):
            pair(hop, step, box, step == 0 and hop == 0).wait_recv()

        def add(part, total):
            for inner in range(depth):
                value = gathered[part, source, box, pl.ds(inner, lines, depth), :]
                total = total + value[:, None, :] * tab[part * depth + inner][None]
            return total

        zeros = jnp.broadcast_to((tab[0] - tab[0])[None], (lines, width, columns))
        cycles[source, box] = lax.fori_loop(0, parts, add, zeros)

    @pl.loop(0, per_peer)
    def _(box):
        arrive(1, box)
        relay(0, box)

    keep_blocks.wait()
    for step in order:
        arrive(step, 0)
    relay(1, 0)
    finish(0, 0)

    @pl.loop(1, per_peer)
    def _(box):
        @pl.when(box + 1 < per_peer)
        def _():
            for step in order:
                far(step, box + 1).start()

        for step in order:
            arrive(step, box)
            relay(step, box - 1)
        relay(1, box)
        finish(0, box)
        finish(1, box - 1)

        @pl.when(box > 1)
        def _():
            for step in order:
                finish(step, box - 2)

    for step in order:
        relay(step, per_peer - 1)
    finish(1, per_peer - 1)
    for back in (2, 1):
        for step in order:
            finish(step, per_peer - back)

    @pl.loop(0, per_peer)
    def _(box):
        for step in range(sub_count):
            if step > 0:
                far(step, box).wait_send()
            for hop in range(1, chips):
                near(hop, step, box, step == 0).wait_send()
            for hop in range(chips):
                pair(hop, step, box, step == 0 and hop == 0).wait_send()

    for step in everyone:
        slot_copy(step).wait()
    keep_slot.wait()


def exchange_all(outgoing, slots, parts, depth, blk_index):
    sub_count, per_peer, rows, columns = outgoing.shape
    chips = parts // 2
    degrees = parts * depth
    width = J // parts
    lines = rows // depth
    polar = own_polar(parts, blk_index)
    log_norm, order, factor, before = legendre_constants(degrees, columns)
    diag = jnp.exp(log_norm + order * jnp.log(jnp.sin(polar))[:, None])
    cosines = jnp.broadcast_to(jnp.cos(polar)[:, None], (width, columns))
    dma = pltpu.SemaphoreType.DMA
    anywhere = pl.BlockSpec(memory_space=pl.ANY)
    vmem = pl.BlockSpec(memory_space=pltpu.VMEM)
    hops = max(chips - 1, 1)
    return pl.pallas_call(
        functools.partial(exchange, sub_count, chips),
        out_shape=(
            jax.ShapeDtypeStruct((sub_count, per_peer, lines, width, columns), jnp.float32),
            jax.ShapeDtypeStruct(slots.shape, jnp.int32),
        ),
        in_specs=[anywhere] + [vmem] * 6,
        out_specs=(vmem, vmem),
        scratch_shapes=[
            pltpu.VMEM((parts, sub_count, per_peer, rows, columns), jnp.float32),
            pltpu.VMEM((degrees, width, columns), jnp.float32),
            dma((sub_count, per_peer)),
            dma((sub_count, per_peer)),
            dma((hops, sub_count, per_peer)),
            dma((hops, sub_count, per_peer)),
            dma((chips, sub_count, per_peer)),
            dma((chips, sub_count, per_peer)),
            dma((sub_count,)),
            dma((sub_count,)),
            dma((2,)),
        ],
        compiler_params=pltpu.CompilerParams(
            collective_id=0, has_side_effects=True, vmem_limit_bytes=40 * 1024 * 1024
        ),
        name="exchange",
    )(
        outgoing,
        slots,
        diag,
        cosines,
        jnp.asarray(order),
        jnp.asarray(factor),
        jnp.asarray(before),
    )


def body(coefficients, owner_slot, child_list):
    box_count, cases, _, depth, columns = coefficients.shape
    sub_count = lax.axis_size("sub")
    parts = lax.axis_size("blk")
    per_peer = box_count // sub_count
    targets = owner_slot // box_count
    positions = owner_slot % box_count
    send_order = jnp.argsort(targets, stable=True)
    flat = coefficients.reshape(box_count, cases * 2 * depth, columns)
    outgoing = flat[send_order].reshape(sub_count, per_peer, cases * 2 * depth, columns)
    slots = positions[send_order].reshape(sub_count, 1, per_peer)
    slots = jnp.pad(slots, ((0, 0), (0, 0), (0, 128 - per_peer)))
    blk_index = lax.axis_index("blk")
    cycles, placed = exchange_all(outgoing, slots, parts, depth, blk_index)
    source = jnp.argsort(placed[:, 0, :per_peer].reshape(-1)).astype(jnp.int32)
    cycles = cycles.reshape((box_count,) + cycles.shape[2:])
    return make_children(cycles, source, child_list, parts, 2 * cases, blk_index)


def solution(mesh):
    placed = (P("sub", None, None, "blk", None), P("sub"), P("sub", None))
    return jax.shard_map(
        body,
        mesh=mesh,
        in_specs=placed,
        out_specs=P("sub", None, None, "blk", None, None),
        check_vma=False,
    )
```

profile of v0, /device:TPU:0, one launch (start us, length us, event | category | flops | bytes accessed | tf_op | source)
XLA Modules:
  0.0 154.0 jit_solution(11493722510023593171)
XLA Ops:
  0.1 0.1 fusion.4
  0.2 0.7 and_select_fusion
  0.9 2.0 %sort.34 = (s32[64]{0:T(128)}, s32[64]{0:T(128)S(1)}) sort(s32[64]{0:T(128)S(1)} %get-tuple-element.21, s32[64]{0:T(128)S(1)} %iota.34), dimensions={0}, to_apply=%region_0.1 | sort | flops 384 | bytes 1024 | tf_op jit(solution)/shard_map/jit(argsort)/sort | solution.py:422
  3.0 0.8 gather_fusion.1
  3.7 0.1 reshape.110
  3.8 0.1 broadcast_in_dim.9.cosines
  3.9 0.7 broadcast_multiply_fusion.1
  4.7 0.8 copy.11
  5.4 0.1 reshape.111.child
  5.5 0.3 fusion
  6.0 0.0 copy-start.4
  6.0 0.0 copy-start.5
  6.0 0.0 copy-start.6
  6.0 5.0 %gather_fusion = f32[64,128,128]{2,1,0:T(8,128)} fusion(f32[64,128,128]{2,1,0:T(8,128)} %bitcast.14, s32[1024]{0:T(1024)S(1)} %pad_clamp_fusion), kind=kCustom, calls=%fused_computation | custom fusion | bytes 8388864 | tf_op jit(solution)/shard_map/gather | solution.py:424
  11.0 0.0 copy-done.4
  11.0 0.0 copy-done.5
  11.0 0.0 copy-done.6
  11.1 0.0 copy-start.2
  11.1 2.2 %copy-done.2 = f32[64,128,128]{2,1,0:T(8,128)S(1)} copy-done((f32[64,128,128]{2,1,0:T(8,128)S(1)}, f32[64,128,128]{2,1,0:T(8,128)}, u32[]{:S(2)}) %copy-start.2) | copy-done | bytes 4194328
  13.2 0.0 copy-start.3
  13.2 115.7 %exchange.1 = (f32[8,8,8,16,128]{4,3,2,1,0:T(8,128)S(1)}, s32[8,1,128]{2,1,0:T(1,128)S(1)}) custom-call(f32[8,8,128,128]{3,2,1,0:T(8,128)S(1)} %bitcast.11, s32[8,1,128]{2,1,0:T(1,128)S(1)} %pad.4.slots, f32[16,128]{1,0:T(8,128)S(1)} %get-tuple-element.22.diag, f32[16,128]{1,0:T(8,128)S(1)} %broadcast_in_dim.9.cosines, f32[1,128]{1,0:T(1,128)S(1)} %copy-done.6, ...), custom_call_target="tpu_custom_call" | custom-call | tf_op jit(solution)/shard_map/exchange/pallas_call | solution.py:379
  129.0 0.0 copy-start
  129.0 2.0 %copy-done = f32[8,8,8,16,128]{4,3,2,1,0:T(8,128)} copy-done((f32[8,8,8,16,128]{4,3,2,1,0:T(8,128)}, f32[8,8,8,16,128]{4,3,2,1,0:T(8,128)S(1)}, u32[]{:S(2)}) %copy-start) | copy-done | bytes 4194328
  131.0 0.1 reshape_squeeze.3
  131.1 2.1 %sort.35 = (s32[64]{0:T(128)}, s32[64]{0:T(128)S(1)}) sort(s32[64]{0:T(128)S(1)} %reshape_squeeze.3, s32[64]{0:T(128)S(1)} %iota.36), dimensions={0}, to_apply=%region_1.2 | sort | flops 384 | bytes 1024 | tf_op jit(solution)/shard_map/jit(argsort)/sort | solution.py:429
  133.2 0.0 copy-done.3
  133.2 0.0 copy-start.1
  133.2 2.2 %copy-done.1 = f32[8,8,8,16,128]{4,3,2,1,0:T(8,128)S(1)} copy-done((f32[8,8,8,16,128]{4,3,2,1,0:T(8,128)S(1)}, f32[8,8,8,16,128]{4,3,2,1,0:T(8,128)}, u32[]{:S(2)}) %copy-start.1) | copy-done | bytes 4194328
  135.4 18.6 %transform.1 = f32[64,4,8,32,128]{4,3,2,1,0:T(8,128)} custom-call(s32[64]{0:T(128)S(1)} %get-tuple-element.11.source, s32[512]{0:T(512)S(1)} %reshape.111.child, f32[64,8,16,128]{3,2,1,0:T(8,128)S(1)} %bitcast.7, f32[64,8,16,128]{3,2,1,0:T(8,128)S(1)} %bitcast.8, f32[64,8,16,128]{3,2,1,0:T(8,128)S(1)} %bitcast.9, f32[64,8,16,128]{3,2,1,0:T(8,128)S(1)} %bitcast.10, ...), custom_call_target="tpu_custom_call" | custom-call | tf_op jit(solution)/shard_map/transform/pallas_call | solution.py:137
  (13 shorter events, 0.2 us)
Async XLA Ops:
  6.0 5.1 %copy-start.4 = (f32[64,1,128]{2,1,0:T(1,128)S(1)}, f32[64,1,128]{2,1,0:T(1,128)}, u32[]{:S(2)}) copy-start(f32[64,1,128]{2,1,0:T(1,128)} %constant.69.clone.before) | copy-start | bytes 98308
  6.0 5.1 %copy-start.5 = (f32[64,1,128]{2,1,0:T(1,128)S(1)}, f32[64,1,128]{2,1,0:T(1,128)}, u32[]{:S(2)}) copy-start(f32[64,1,128]{2,1,0:T(1,128)} %constant.68.clone.factor) | copy-start | bytes 98308
  6.0 5.0 %copy-start.6 = (f32[1,128]{1,0:T(1,128)S(1)}, f32[1,128]{1,0:T(1,128)}, u32[]{:S(2)}) copy-start(f32[1,128]{1,0:T(1,128)} %constant.66.clone.orders) | copy-start | bytes 1540
  11.1 2.2 %copy-start.2 = (f32[64,128,128]{2,1,0:T(8,128)S(1)}, f32[64,128,128]{2,1,0:T(8,128)}, u32[]{:S(2)}) copy-start(f32[64,128,128]{2,1,0:T(8,128)} %gather_fusion) | copy-start | bytes 12582916
  13.2 120.0 %copy-start.3 = (f32[256,256]{1,0:T(8,128)S(1)}, f32[256,256]{1,0:T(8,128)}, u32[]{:S(2)}) copy-start(f32[256,256]{1,0:T(8,128)} %constant.70.clone.refs_4_) | copy-start | bytes 786436
  129.0 2.0 %copy-start = (f32[8,8,8,16,128]{4,3,2,1,0:T(8,128)}, f32[8,8,8,16,128]{4,3,2,1,0:T(8,128)S(1)}, u32[]{:S(2)}) copy-start(f32[8,8,8,16,128]{4,3,2,1,0:T(8,128)S(1)} %get-tuple-element.12) | copy-start | bytes 12582916
  133.2 2.2 %copy-start.1 = (f32[8,8,8,16,128]{4,3,2,1,0:T(8,128)S(1)}, f32[8,8,8,16,128]{4,3,2,1,0:T(8,128)}, u32[]{:S(2)}) copy-start(f32[8,8,8,16,128]{4,3,2,1,0:T(8,128)} %copy-done) | copy-start | bytes 12582916
where the time goes:
time: 155 us; the launch traced here: 154 us
  Pallas kernels  134 us (86%)
  local copies, waits for them, and re-layouts  13.5 us (9%)
  other arithmetic  6.02 us (4%)
    pallas_call x1, Pallas kernels, exchange_all(): pl.pallas_call(functools.partial(exchange, sub_count, chips), out_shape=(...  116 us
    pallas_call x1, Pallas kernels, make_children(): pl.pallas_call(transform, grid_spec=pltpu.PrefetchScalarGridSpec(num_scal...  18.6 us
    unnamed x15, local copies, waits for them, and re-layouts  7.18 us
    gather x1, local copies, waits for them, and re-layouts, body(): flat[send_order].reshape(sub_count, per_peer, cases * 2 * depth, columns)  5.03 us

commit v1 on v0

v1 whole, which is shorter than its diff:
```python
import functools
import math

import jax
import jax.numpy as jnp
import numpy as np
from jax import lax
from jax.experimental import pallas as pl
from jax.experimental.pallas import tpu as pltpu
from jax.sharding import PartitionSpec as P

J = 64
K = 128
LANES = 128
MIB = 1024 * 1024


def ceil_div(value, by):
    return (value + by - 1) // by


def packed_rows(depth, part):
    return ceil_div(depth * depth * (2 * part + 1), LANES)


def first_lane(depth, part, inner):
    return inner * (2 * depth * part) + inner * inner


def swapped(index, step, size):
    total = 0
    bit = 1
    while bit < size:
        total = total + ((index // bit + step // bit) % 2) * bit
        bit *= 2
    return total


def legendre_constants(degrees, columns, parts):
    order = np.abs(np.arange(columns) - degrees).astype(np.float64)
    log_norm = np.array(
        [
            0.5
            * (
                math.log((2 * v + 1) / (4 * math.pi))
                + math.lgamma(2 * v + 1)
                - v * math.log(4.0)
                - 2 * math.lgamma(v + 1)
            )
            for v in order
        ]
    )
    polar = np.pi * (np.arange(J) + 0.5) / J
    diag = np.exp(log_norm[None] + order[None] * np.log(np.sin(polar))[:, None])
    cosines = np.broadcast_to(np.cos(polar)[:, None], (J, columns))
    level = np.arange(degrees, dtype=np.float64)[:, None]
    factor = np.sqrt(np.maximum(4 * level * level - 1, 1.0) / np.maximum(level * level - order[None] ** 2, 1.0))
    before = np.ones_like(factor)
    before[1:] = 1.0 / factor[:-1]
    shape = (parts, J // parts, columns)
    return (
        diag.astype(np.float32).reshape(shape),
        cosines.astype(np.float32).reshape(shape),
        order.astype(np.float32)[None],
        factor.astype(np.float32)[:, None, :],
        before.astype(np.float32)[:, None, :],
    )


def wave_matrix(degrees, columns, azimuths):
    turns = ((np.arange(columns)[:, None] - degrees) * np.arange(azimuths)[None, :]) % azimuths
    angle = 2.0 * np.pi * turns / azimuths
    cosine, sine = np.cos(angle), np.sin(angle)
    upper = np.concatenate([cosine, sine], axis=1)
    lower = np.concatenate([-sine, cosine], axis=1)
    return np.concatenate([upper, lower], axis=0).astype(np.float32)


def phase_tables(parts, azimuths):
    polar = np.pi * (np.arange(J) + 0.5) / J
    azimuth = 2.0 * np.pi * np.arange(azimuths) / azimuths
    octants = np.arange(8)
    sign = [(2 * (octants >> bit & 1) - 1).astype(np.float64)[:, None, None] for bit in range(3)]
    dir_x = np.sin(polar)[:, None] * np.cos(azimuth)[None, :]
    dir_y = np.sin(polar)[:, None] * np.sin(azimuth)[None, :]
    dir_z = np.cos(polar)[:, None] * np.ones_like(azimuth)[None, :]
    phase = 5.5 * (sign[0] * dir_x + sign[1] * dir_y + sign[2] * dir_z)

    def per_part(values):
        twice = np.repeat(values, 2, axis=1).astype(np.float32)
        return twice.reshape(8, parts, 2 * J // parts, azimuths).transpose(1, 0, 2, 3)

    return per_part(np.cos(phase)), per_part(np.sin(phase))


def pack(slot, source, out, placed, stage, count):
    step = pl.program_id(0)
    blk = lax.axis_index("blk")
    boxes, depth_lines, columns = source.shape
    sub_count, groups, rows, each, lines, _ = out.shape
    depth = depth_lines // lines
    total = sub_count * groups * each

    @pl.when(step == 0)
    def _():
        stage[...] = jnp.zeros_like(stage)
        placed[...] = jnp.zeros_like(placed)
        for sub in range(sub_count):
            count[sub] = 0

    lane = lax.broadcasted_iota(jnp.int32, (boxes, lines, columns), 2)
    for inner in range(depth):
        degree = depth * blk + inner
        begin = first_lane(depth, blk, inner)
        row, offset = begin // LANES, begin % LANES
        end = offset + 2 * degree + 1
        value = source[:, pl.ds(inner, lines, depth), :]
        value = pltpu.roll(value, (offset + LANES + degree - columns // 2) % LANES, 2)
        here = (lane >= offset) & (lane < end)
        stage[row] = jnp.where(here, value, stage[row])
        stage[row + 1] = jnp.where(lane < end - LANES, value, stage[row + 1])

    slot_lane = lax.broadcasted_iota(jnp.int32, (1, LANES), 1)
    for box in range(boxes):
        own = slot[step * boxes + box]
        target = own // total
        rank = count[target]
        count[target] = rank + 1
        out[target, rank // each, :, rank % each] = stage[pl.ds(0, rows), box]
        placed[target] = jnp.where(slot_lane == rank, own % total, placed[target])


def fill_table(tab, diag, cosines, order_ref, factor_ref, before_ref):
    degrees, width, lines, columns = tab.shape
    order = jnp.broadcast_to(order_ref[...], diag.shape)
    next_value = jnp.sqrt(2.0 * order + 3.0) * cosines * diag

    def advance(degree, state):
        previous, before = state
        level = lax.convert_element_type(degree, jnp.float32)
        recur = factor_ref[degree] * (cosines * previous - before * before_ref[degree])
        value = jnp.where(level == order + 1.0, next_value, recur)
        value = jnp.where(level == order, diag, value)
        value = jnp.where(level < order, 0.0, value)
        tab[degree] = jnp.broadcast_to(value[:, None, :], (width, lines, columns))
        return value, previous

    zeros = diag - diag
    lax.fori_loop(0, degrees, advance, (zeros, zeros))


def exchange(
    blocks,
    slots,
    diag,
    cosines,
    orders,
    factor,
    before,
    high,
    low,
    waves,
    quarters,
    source_of,
    placed,
    gathered,
    tab,
    cycles,
    send_far,
    recv_far,
    send_near,
    recv_near,
    send_pair,
    recv_pair,
    send_slot,
    recv_slot,
    local,
):
    sub_count, groups, _, each, lines, columns = blocks.shape
    degrees, width, _, _ = tab.shape
    parts = diag.shape[0]
    chips = parts // 2
    depth = degrees // parts
    cases = lines // 2
    sizes = [packed_rows(depth, part) for part in range(parts)]
    starts = [sum(sizes[:part]) for part in range(parts)]
    sub = lax.axis_index("sub")
    blk = lax.axis_index("blk")
    chip = blk // 2
    core = blk % 2
    sibling = chip * 2 + (1 - core)

    def start_of(part):
        total = 0
        for before_part in range(parts - 1):
            total = total + jnp.where(part > before_part, sizes[before_part], 0)
        return total

    def sized(part, action):
        rows = packed_rows(depth, part)
        for size in sorted(set(sizes)):
            pl.when(rows == size)(functools.partial(action, size))

    def remote(source, target, send, recv, device):
        return pltpu.make_async_remote_copy(
            src_ref=source,
            dst_ref=target,
            send_sem=send,
            recv_sem=recv,
            device_id=device,
            device_id_type=pl.DeviceIdType.MESH,
        )

    own_rows = start_of(blk)

    def held(hop, of_core):
        return ((chip + chips - hop) % chips) * 2 + of_core

    def far(step, group, size):
        peer = swapped(sub, step, sub_count)
        return remote(
            blocks.at[peer, group, pl.ds(0, size)],
            gathered.at[sub, group, pl.ds(own_rows, size)],
            send_far.at[step, group],
            recv_far.at[step, group],
            (peer, blk),
        )

    def slot_copy(step):
        peer = swapped(sub, step, sub_count)
        return remote(slots.at[peer], placed.at[sub], send_slot.at[step], recv_slot.at[step], (peer, blk))

    def near(hop, step, group, part, size, own=False):
        source = swapped(sub, step, sub_count)
        rows = pl.ds(start_of(part), size)
        return remote(
            blocks.at[sub, group, pl.ds(0, size)] if own else gathered.at[source, group, rows],
            gathered.at[source, group, rows],
            send_near.at[hop - 1, step, group],
            recv_near.at[hop - 1, step, group],
            (sub, ((chip + hop) % chips) * 2 + core),
        )

    def pair(hop, step, group, part, size, own=False):
        source = swapped(sub, step, sub_count)
        rows = pl.ds(start_of(part), size)
        return remote(
            blocks.at[sub, group, pl.ds(0, size)] if own else gathered.at[source, group, rows],
            gathered.at[source, group, rows],
            send_pair.at[hop, step, group],
            recv_pair.at[hop, step, group],
            (sub, sibling),
        )

    def keep(group, size):
        return pltpu.make_async_copy(
            blocks.at[sub, group, pl.ds(0, size)],
            gathered.at[sub, group, pl.ds(own_rows, size)],
            local.at[group],
        )

    barrier = pltpu.get_barrier_semaphore()

    def greet(device):
        pl.semaphore_signal(barrier, inc=1, device_id=device, device_id_type=pl.DeviceIdType.MESH)

    for step in range(1, sub_count):
        greet((swapped(sub, step, sub_count), blk))
    for hop in range(1, chips):
        greet((sub, ((chip + hop) % chips) * 2 + core))
    greet((sub, sibling))
    pl.semaphore_wait(barrier, sub_count - 1 + chips)

    others = sub_count - 1

    def step_at(index):
        return 1 + (index + sub_count // 2 - 1) % others

    for step in range(1, sub_count):
        slot_copy(step).start()
    keep_slot = pltpu.make_async_copy(slots.at[sub], placed.at[sub], local.at[groups])
    keep_slot.start()

    def begin(size):
        @pl.loop(0, groups)
        def _(group):
            for hop in range(1, chips):
                near(hop, 0, group, blk, size, True).start()

            @pl.loop(0, others)
            def _(index):
                far(step_at(index), group, size).start()

            pair(0, 0, group, blk, size, True).start()
            keep(group, size).start()

    sized(blk, begin)
    fill_table(tab, diag[blk], cosines[blk], orders, factor, before)

    lane = lax.broadcasted_iota(jnp.int32, (each, lines, columns), 2)

    def relay(step, group):
        def act(size):
            far(step, group, size).wait_recv()
            for hop in range(1, chips):
                near(hop, step, group, blk, size).start()
            pair(0, step, group, blk, size).start()

        sized(blk, act)

    def hand_on(step, group):
        for hop in range(1, chips):
            part = held(hop, core)

            def act(size):
                near(hop, step, group, part, size).wait_recv()
                pair(hop, step, group, part, size).start()

            sized(part, act)

    def finish(step, group):
        for hop in range(chips):
            part = held(hop, 1 - core)
            sized(part, lambda size: pair(hop, step, group, part, size).wait_recv())
        source = swapped(sub, step, sub_count)
        totals = [jnp.zeros((width, lines, columns), jnp.float32) for _ in range(each)]
        for degree in range(degrees):
            part, inner = degree // depth, degree % depth
            begin = first_lane(depth, part, inner)
            row, offset = starts[part] + begin // LANES, begin % LANES
            value = gathered[source, group, row]
            if offset + 2 * degree + 1 > LANES:
                value = jnp.where(lane >= offset, value, gathered[source, group, row + 1])
            shift = (columns // 2 - degree - offset) % LANES
            if shift:
                value = pltpu.roll(value, shift, 2)
            for box in range(each):
                totals[box] = totals[box] + value[box][None] * tab[degree]
        for box in range(each):
            for index in range(width):
                cycles[pl.ds(box * lines * width + index, lines, width), :] = totals[box][index]
        both = cycles[...].reshape(each * cases, 2, width, columns)
        rows = each * cases * width
        both = jnp.concatenate([both[:, 0].reshape(rows, columns), both[:, 1].reshape(rows, columns)], axis=1)
        top = both.astype(jnp.bfloat16)
        rest = (both - top.astype(jnp.float32)).astype(jnp.bfloat16)
        dot = functools.partial(jnp.dot, preferred_element_type=jnp.float32)
        wave = dot(rest, high[...]) + dot(top, low[...]) + dot(top, high[...])
        real, imag = wave[:, :K], wave[:, K:]
        for box in range(each):
            for case in range(cases):
                at = slice((box * cases + case) * width, (box * cases + case + 1) * width)
                waves[source, group, box, case, pl.ds(0, width, 2), :] = real[at]
                waves[source, group, box, case, pl.ds(1, width, 2), :] = imag[at]
                quarters[source, group, box, case, pl.ds(0, width, 2), :] = -imag[at]
                quarters[source, group, box, case, pl.ds(1, width, 2), :] = real[at]

    def waits_keep(size):
        @pl.loop(0, groups)
        def _(group):
            keep(group, size).wait()

    sized(blk, waits_keep)

    chunks = sub_count * groups
    near_lag, pair_lag = 2, 4

    def place_of(chunk):
        later = chunk - groups
        own = chunk < groups
        step = jnp.where(own, 0, step_at(later % others))
        group = jnp.where(own, chunk, later // others)
        return step, group

    @pl.loop(0, chunks + pair_lag)
    def _(chunk):
        @pl.when((chunk >= groups) & (chunk < chunks))
        def _():
            relay(*place_of(chunk))

        @pl.when(chunk >= pair_lag)
        def _():
            finish(*place_of(chunk - pair_lag))

        @pl.when((chunk >= near_lag) & (chunk < chunks + near_lag))
        def _():
            hand_on(*place_of(chunk - near_lag))

    def drain(step, group):
        def own_act(size):
            @pl.when(step > 0)
            def _():
                far(step, group, size).wait_send()

            for hop in range(1, chips):
                near(hop, step, group, blk, size).wait_send()
            pair(0, step, group, blk, size).wait_send()

        sized(blk, own_act)
        for hop in range(1, chips):
            part = held(hop, core)
            sized(part, lambda size: pair(hop, step, group, part, size).wait_send())

    @pl.loop(0, chunks)
    def _(chunk):
        drain(*place_of(chunk))

    for step in range(1, sub_count):
        slot_copy(step).wait()
    keep_slot.wait()
    per_peer = groups * each
    turned = jnp.transpose(placed[:, 0, :])
    where = lax.broadcasted_iota(jnp.int32, (per_peer, LANES), 1)
    rank = lax.broadcasted_iota(jnp.int32, (per_peer, LANES), 0)
    found = jnp.zeros((1, LANES), jnp.int32)
    for source in range(sub_count):
        slot = turned[:per_peer, source : source + 1]
        hit = jnp.where(slot == where, rank + source * per_peer, 0)
        found = found + jnp.sum(hit, axis=0, keepdims=True)
    source_of[...] = found


def phases(source_of, octants, waves, quarters, phase_cos, phase_sin, out):
    step = pl.program_id(0)
    count, cases, places, _, _ = out.shape
    for box in range(count):
        at = step * count + box
        source = source_of[at]
        for place in range(places):
            octant = octants[place, at]
            turn_cos = phase_cos[0, octant]
            turn_sin = phase_sin[0, octant]
            for case in range(cases):
                out[box, case, place] = waves[source, case] * turn_cos + quarters[source, case] * turn_sin


def body(coefficients, owner_slot, child_list):
    boxes, cases, _, depth, columns = coefficients.shape
    sub_count = lax.axis_size("sub")
    parts = lax.axis_size("blk")
    degrees = parts * depth
    width = J // parts
    lines = cases * 2
    per_peer = boxes // sub_count
    each = 2 if per_peer % 2 == 0 else 1
    groups = per_peer // each
    chips = parts // 2
    hops = max(chips - 1, 1)
    rows = max(packed_rows(depth, part) for part in range(parts))
    total_rows = sum(packed_rows(depth, part) for part in range(parts))
    vmem = pl.BlockSpec(memory_space=pltpu.VMEM)
    at_once = 8
    outgoing, slots = pl.pallas_call(
        pack,
        grid_spec=pltpu.PrefetchScalarGridSpec(
            num_scalar_prefetch=1,
            grid=(boxes // at_once,),
            in_specs=[pl.BlockSpec((at_once, lines * depth, columns), lambda i, slot: (i, 0, 0))],
            out_specs=(vmem, vmem),
            scratch_shapes=[
                pltpu.VMEM((rows + 1, at_once, lines, columns), jnp.float32),
                pltpu.SMEM((sub_count,), jnp.int32),
            ],
        ),
        out_shape=(
            jax.ShapeDtypeStruct((sub_count, groups, rows, each, lines, columns), jnp.float32),
            jax.ShapeDtypeStruct((sub_count, 1, LANES), jnp.int32),
        ),
        compiler_params=pltpu.CompilerParams(vmem_limit_bytes=12 * MIB),
        name="pack",
    )(owner_slot, coefficients.reshape(boxes, lines * depth, columns))

    matrix = wave_matrix(degrees, columns, K)
    high = matrix.astype(jnp.bfloat16)
    low = (matrix - high.astype(np.float32)).astype(jnp.bfloat16)
    dma = pltpu.SemaphoreType.DMA
    waves, quarters, source_of = pl.pallas_call(
        exchange,
        out_shape=(
            jax.ShapeDtypeStruct((sub_count, groups, each, cases, 2 * width, K), jnp.float32),
            jax.ShapeDtypeStruct((sub_count, groups, each, cases, 2 * width, K), jnp.float32),
            jax.ShapeDtypeStruct((1, LANES), jnp.int32),
        ),
        in_specs=[vmem] * 9,
        out_specs=(vmem, vmem, vmem),
        scratch_shapes=[
            pltpu.VMEM((sub_count, 1, LANES), jnp.int32),
            pltpu.VMEM((sub_count, groups, total_rows, each, lines, columns), jnp.float32),
            pltpu.VMEM((degrees, width, lines, columns), jnp.float32),
            pltpu.VMEM((each * lines * width, columns), jnp.float32),
            dma((sub_count, groups)),
            dma((sub_count, groups)),
            dma((hops, sub_count, groups)),
            dma((hops, sub_count, groups)),
            dma((chips, sub_count, groups)),
            dma((chips, sub_count, groups)),
            dma((sub_count,)),
            dma((sub_count,)),
            dma((groups + 1,)),
        ],
        compiler_params=pltpu.CompilerParams(
            collective_id=0, has_side_effects=True, vmem_limit_bytes=40 * MIB
        ),
        name="exchange",
    )(
        outgoing,
        slots,
        *(jnp.asarray(constant) for constant in legendre_constants(degrees, columns, parts)),
        jnp.asarray(high),
        jnp.asarray(low),
    )

    phase_cos, phase_sin = phase_tables(parts, K)
    blk = lax.axis_index("blk").astype(jnp.int32)
    count = 2
    own = pl.BlockSpec((1, 8, 2 * width, K), lambda i, source, octants, part: (part[0], 0, 0, 0))
    out = pl.pallas_call(
        lambda source, octants, part, *refs: phases(source, octants, *refs),
        grid_spec=pltpu.PrefetchScalarGridSpec(
            num_scalar_prefetch=3,
            grid=(boxes // count,),
            in_specs=[vmem, vmem, own, own],
            out_specs=pl.BlockSpec(
                (count, cases, 8, 2 * width, K), lambda i, source, octants, part: (i, 0, 0, 0, 0)
            ),
        ),
        out_shape=jax.ShapeDtypeStruct((boxes, cases, 8, 2 * width, K), jnp.float32),
        compiler_params=pltpu.CompilerParams(vmem_limit_bytes=32 * MIB),
        name="phases",
    )(
        source_of.reshape(-1),
        child_list.T,
        blk.reshape(1),
        waves.reshape(boxes, cases, 2 * width, K),
        quarters.reshape(boxes, cases, 2 * width, K),
        jnp.asarray(phase_cos),
        jnp.asarray(phase_sin),
    )
    return out.reshape(boxes, cases, 8, width, 2, K)


def solution(mesh):
    placed = (P("sub", None, None, "blk", None), P("sub"), P("sub", None))
    return jax.shard_map(
        body,
        mesh=mesh,
        in_specs=placed,
        out_specs=P("sub", None, None, "blk", None, None),
        check_vma=False,
    )
```

time: 155 us -> 128 us (0.83)
  the two profiles are of different devices: /device:TPU:0 before, /device:TPU:9 now
where the time goes in v1:
time: 128 us
  Pallas kernels  125 us (98%)
  local copies, waits for them, and re-layouts  2.92 us (2%)
    pallas_call x1, Pallas kernels, body(): pl.pallas_call(exchange, out_shape=(jax.ShapeDtypeStruct((sub_count, grou...  102 us
    pallas_call x1, Pallas kernels, body(): pl.pallas_call(lambda source, octants, part, *refs: phases(source, octant...  18.3 us
    pallas_call x1, Pallas kernels, body(): pl.pallas_call(pack, grid_spec=pltpu.PrefetchScalarGridSpec(num_scalar_pr...  3.83 us
    unnamed x24, local copies, waits for them, and re-layouts  2.92 us

profile of v1, /device:TPU:9, one launch (start us, length us, event | category | flops | bytes accessed | tf_op | source)
XLA Modules:
  0.0 127.6 jit_solution(8361928290001442247)
XLA Ops:
  0.0 0.0 copy-start.11
  0.0 0.0 copy-start.9
  0.0 0.0 copy-start
  0.0 2.2 %copy-done = f32[64,4,2,16,128]{4,3,2,1,0:T(8,128)S(1)} copy-done((f32[64,4,2,16,128]{4,3,2,1,0:T(8,128)S(1)}, f32[64,4,2,16,128]{4,3,2,1,0:T(8,128)}, u32[]{:S(2)}) %copy-start) | copy-done | bytes 4194328
  2.2 0.0 copy-start.10
  2.2 0.7 copy-done.10
  2.9 0.0 copy-start.3
  2.9 0.0 copy-start.4
  2.9 0.0 copy-start.5
  2.9 0.0 copy-start.6
  2.9 0.0 copy-start.7
  2.9 0.0 copy-start.8
  2.9 0.0 copy-start.1
  2.9 0.0 copy-start.2
  2.9 3.8 %pack.1 = (f32[8,4,14,2,8,128]{5,4,3,2,1,0:T(8,128)S(1)}, s32[8,1,128]{2,1,0:T(1,128)S(1)}) custom-call(s32[64]{0:T(128)S(1)} %copy-done.10, f32[64,128,128]{2,1,0:T(8,128)S(1)} %bitcast.9), custom_call_target="tpu_custom_call" | custom-call | tf_op jit(solution)/shard_map/pack/pallas_call | solution.py:453
  6.8 0.0 copy-done.11
  6.8 0.0 copy-done.3
  6.8 0.0 copy-done.4
  6.8 0.0 copy-done.5
  6.8 0.0 copy-done.6
  6.8 0.0 copy-done.7
  6.8 0.0 copy-done.8
  6.8 102.4 %exchange.1 = (f32[8,4,2,4,32,128]{5,4,3,2,1,0:T(8,128)S(1)}, f32[8,4,2,4,32,128]{5,4,3,2,1,0:T(8,128)S(1)}, s32[1,128]{1,0:T(1,128)S(1)}) custom-call(f32[8,4,14,2,8,128]{5,4,3,2,1,0:T(8,128)S(1)} %get-tuple-element.10.blocks, s32[8,1,128]{2,1,0:T(1,128)S(1)} %get-tuple-element.11.slots, f32[4,16,128]{2,1,0:T(8,128)S(1)} %copy-done.8, ...), custom_call_target="tpu_custom_call" | custom-call | tf_op jit(solution)/shard_map/exchange/pallas_call | solution.py:477
  109.3 0.0 copy-done.9
  109.3 0.0 copy-done.1
  109.3 0.0 copy-done.2
  109.3 18.3 %phases.1 = f32[64,4,8,32,128]{4,3,2,1,0:T(8,128)} custom-call(s32[128]{0:T(128)S(1)} %bitcast.11, s32[8,64]{1,0:T(8,128)S(1)} %bitcast.10, s32[1]{0:T(128)} %bitcast.3.part, f32[64,4,32,128]{3,2,1,0:T(8,128)S(1)} %bitcast.7, f32[64,4,32,128]{3,2,1,0:T(8,128)S(1)} %bitcast.8, f32[4,8,32,128]{3,2,1,0:T(8,128)S(1)} %copy-done.2, f32[4,8,32,128]{3,2,1,0:T(8,128)S(1)} %copy-done.1), custom_call_target="tpu_custom_call" | custom-call | tf_op jit(solution)/shard_map/phases/pallas_call | solution.py:517
Async XLA Ops:
  0.0 6.8 %copy-start.11 = (f32[1,128]{1,0:T(1,128)S(1)}, f32[1,128]{1,0:T(1,128)}, u32[]{:S(2)}) copy-start(f32[1,128]{1,0:T(1,128)} %constant.24.clone.orders) | copy-start | bytes 1540
  0.0 109.3 %copy-start.9 = (s32[64,8]{0,1:T(8,128)S(1)}, s32[64,8]{0,1:T(8,128)}, u32[]{:S(2)}) copy-start(s32[64,8]{0,1:T(8,128)} %param.14) | copy-start | bytes 6148
  0.0 2.2 %copy-start = (f32[64,4,2,16,128]{4,3,2,1,0:T(8,128)S(1)}, f32[64,4,2,16,128]{4,3,2,1,0:T(8,128)}, u32[]{:S(2)}) copy-start(f32[64,4,2,16,128]{4,3,2,1,0:T(8,128)} %param.12) | copy-start | bytes 12582916
  2.2 0.7 copy-start.10
  2.9 3.9 %copy-start.3 = (bf16[256,256]{1,0:T(8,128)(2,1)S(1)}, bf16[256,256]{1,0:T(8,128)(2,1)}, u32[]{:S(2)}) copy-start(bf16[256,256]{1,0:T(8,128)(2,1)} %constant.28.clone.low) | copy-start | bytes 393220
  2.9 3.9 %copy-start.4 = (bf16[256,256]{1,0:T(8,128)(2,1)S(1)}, bf16[256,256]{1,0:T(8,128)(2,1)}, u32[]{:S(2)}) copy-start(bf16[256,256]{1,0:T(8,128)(2,1)} %constant.27.clone.high) | copy-start | bytes 393220
  2.9 3.9 %copy-start.5 = (f32[64,1,128]{2,1,0:T(1,128)S(1)}, f32[64,1,128]{2,1,0:T(1,128)}, u32[]{:S(2)}) copy-start(f32[64,1,128]{2,1,0:T(1,128)} %constant.26.clone.before) | copy-start | bytes 98308
  2.9 3.9 %copy-start.6 = (f32[64,1,128]{2,1,0:T(1,128)S(1)}, f32[64,1,128]{2,1,0:T(1,128)}, u32[]{:S(2)}) copy-start(f32[64,1,128]{2,1,0:T(1,128)} %constant.25.clone.factor) | copy-start | bytes 98308
  2.9 3.9 %copy-start.7 = (f32[4,16,128]{2,1,0:T(8,128)S(1)}, f32[4,16,128]{2,1,0:T(8,128)}, u32[]{:S(2)}) copy-start(f32[4,16,128]{2,1,0:T(8,128)} %constant.23.clone.cosines) | copy-start | bytes 98308
  2.9 3.9 %copy-start.8 = (f32[4,16,128]{2,1,0:T(8,128)S(1)}, f32[4,16,128]{2,1,0:T(8,128)}, u32[]{:S(2)}) copy-start(f32[4,16,128]{2,1,0:T(8,128)} %constant.22.clone.diag) | copy-start | bytes 98308
  2.9 106.4 %copy-start.1 = (f32[4,8,32,128]{3,2,1,0:T(8,128)S(1)}, f32[4,8,32,128]{3,2,1,0:T(8,128)}, u32[]{:S(2)}) copy-start(f32[4,8,32,128]{3,2,1,0:T(8,128)} %constant.30.clone.refs_3_) | copy-start | bytes 1572868
  2.9 106.4 %copy-start.2 = (f32[4,8,32,128]{3,2,1,0:T(8,128)S(1)}, f32[4,8,32,128]{3,2,1,0:T(8,128)}, u32[]{:S(2)}) copy-start(f32[4,8,32,128]{3,2,1,0:T(8,128)} %constant.29.clone.refs_2_) | copy-start | bytes 1572868

commit v2 on v1

--- a/solution.py
+++ b/solution.py
@@ -93,41 +93,46 @@
     return per_part(np.cos(phase)), per_part(np.sin(phase))
 
 
-def pack(slot, source, out, placed, stage, count):
-    step = pl.program_id(0)
+def pack(slot, source, out, placed, stage, count, arrived, sems):
     blk = lax.axis_index("blk")
-    boxes, depth_lines, columns = source.shape
+    _, at_once, depth_lines, columns = arrived.shape
     sub_count, groups, rows, each, lines, _ = out.shape
     depth = depth_lines // lines
     total = sub_count * groups * each
-
-    @pl.when(step == 0)
-    def _():
-        stage[...] = jnp.zeros_like(stage)
-        placed[...] = jnp.zeros_like(placed)
-        for sub in range(sub_count):
-            count[sub] = 0
-
-    lane = lax.broadcasted_iota(jnp.int32, (boxes, lines, columns), 2)
-    for inner in range(depth):
-        degree = depth * blk + inner
-        begin = first_lane(depth, blk, inner)
-        row, offset = begin // LANES, begin % LANES
-        end = offset + 2 * degree + 1
-        value = source[:, pl.ds(inner, lines, depth), :]
-        value = pltpu.roll(value, (offset + LANES + degree - columns // 2) % LANES, 2)
-        here = (lane >= offset) & (lane < end)
-        stage[row] = jnp.where(here, value, stage[row])
-        stage[row + 1] = jnp.where(lane < end - LANES, value, stage[row + 1])
-
+    steps = total // at_once
+
+    def fetch(step):
+        return pltpu.make_async_copy(source.at[pl.ds(step * at_once, at_once)], arrived.at[step], sems.at[step])
+
+    for step in range(steps):
+        fetch(step).start()
+    stage[...] = jnp.zeros_like(stage)
+    placed[...] = jnp.zeros_like(placed)
+    for sub in range(sub_count):
+        count[sub] = 0
+    lane = lax.broadcasted_iota(jnp.int32, (at_once, lines, columns), 2)
     slot_lane = lax.broadcasted_iota(jnp.int32, (1, LANES), 1)
-    for box in range(boxes):
-        own = slot[step * boxes + box]
-        target = own // total
-        rank = count[target]
-        count[target] = rank + 1
-        out[target, rank // each, :, rank % each] = stage[pl.ds(0, rows), box]
-        placed[target] = jnp.where(slot_lane == rank, own % total, placed[target])
+
+    @pl.loop(0, steps)
+    def _(step):
+        fetch(step).wait()
+        for inner in range(depth):
+            degree = depth * blk + inner
+            begin = first_lane(depth, blk, inner)
+            row, offset = begin // LANES, begin % LANES
+            end = offset + 2 * degree + 1
+            value = arrived[step, :, pl.ds(inner, lines, depth), :]
+            value = pltpu.roll(value, (offset + LANES + degree - columns // 2) % LANES, 2)
+            here = (lane >= offset) & (lane < end)
+            stage[row] = jnp.where(here, value, stage[row])
+            stage[row + 1] = jnp.where(lane < end - LANES, value, stage[row + 1])
+        for box in range(at_once):
+            own = slot[step * at_once + box]
+            target = own // total
+            rank = count[target]
+            count[target] = rank + 1
+            out[target, rank // each, :, rank % each] = stage[pl.ds(0, rows), box]
+            placed[target] = jnp.where(slot_lane == rank, own % total, placed[target])
 
 
 def fill_table(tab, diag, cosines, order_ref, factor_ref, before_ref):
@@ -175,6 +180,11 @@
     send_slot,
     recv_slot,
     local,
+    transit,
+    send_early,
+    recv_early,
+    send_far2,
+    recv_far2,
 ):
     sub_count, groups, _, each, lines, columns = blocks.shape
     degrees, width, _, _ = tab.shape
@@ -212,6 +222,29 @@
         )
 
     own_rows = start_of(blk)
+    feeds = blk == parts - 1 if chips == 2 else None
+    forwards = blk == parts - 3 if chips == 2 else None
+    heavy, heavy_rows = sizes[-1], starts[-1]
+
+    def early(step, group):
+        peer = swapped(sub, step, sub_count)
+        return remote(
+            blocks.at[peer, group, pl.ds(0, heavy)],
+            transit.at[step, group],
+            send_early.at[step, group],
+            recv_early.at[step, group],
+            (sub, parts - 3),
+        )
+
+    def far2(step, group):
+        peer = swapped(sub, step, sub_count)
+        return remote(
+            transit.at[step, group],
+            gathered.at[sub, group, pl.ds(heavy_rows, heavy)],
+            send_far2.at[step, group],
+            recv_far2.at[step, group],
+            (peer, blk),
+        )
 
     def held(hop, of_core):
         return ((chip + chips - hop) % chips) * 2 + of_core
@@ -272,6 +305,7 @@
     pl.semaphore_wait(barrier, sub_count - 1 + chips)
 
     others = sub_count - 1
+    ahead = 1
 
     def step_at(index):
         return 1 + (index + sub_count // 2 - 1) % others
@@ -282,19 +316,31 @@
     keep_slot.start()
 
     def begin(size):
+        @pl.loop(0, min(ahead, groups))
+        def _(group):
+            @pl.loop(0, others)
+            def _(index):
+                far(step_at(index), group, size).start()
+
         @pl.loop(0, groups)
         def _(group):
             for hop in range(1, chips):
                 near(hop, 0, group, blk, size, True).start()
 
-            @pl.loop(0, others)
-            def _(index):
-                far(step_at(index), group, size).start()
-
             pair(0, 0, group, blk, size, True).start()
             keep(group, size).start()
 
     sized(blk, begin)
+    if chips == 2:
+
+        @pl.when(feeds)
+        def _():
+            @pl.loop(0, groups)
+            def _(group):
+                @pl.loop(0, others)
+                def _(index):
+                    early(step_at(index), group).start()
+
     fill_table(tab, diag[blk], cosines[blk], orders, factor, before)
 
     lane = lax.broadcasted_iota(jnp.int32, (each, lines, columns), 2)
@@ -302,18 +348,42 @@
     def relay(step, group):
         def act(size):
             far(step, group, size).wait_recv()
-            for hop in range(1, chips):
-                near(hop, step, group, blk, size).start()
+            if chips != 2:
+                for hop in range(1, chips):
+                    near(hop, step, group, blk, size).start()
+            elif size != heavy:
+                near(1, step, group, blk, size).start()
             pair(0, step, group, blk, size).start()
 
+            @pl.when(group + ahead < groups)
+            def _():
+                far(step, group + ahead, size).start()
+
         sized(blk, act)
+
+    def forward(step, group):
+        @pl.when(forwards)
+        def _():
+            early(step, group).wait_recv()
+            far2(step, group).start()
 
     def hand_on(step, group):
         for hop in range(1, chips):
             part = held(hop, core)
 
             def act(size):
-                near(hop, step, group, part, size).wait_recv()
+                if chips == 2 and size == heavy:
+
+                    @pl.when(step > 0)
+                    def _():
+                        far2(step, group).wait_recv()
+
+                    @pl.when(step == 0)
+                    def _():
+                        near(hop, step, group, part, size).wait_recv()
+
+                else:
+                    near(hop, step, group, part, size).wait_recv()
                 pair(hop, step, group, part, size).start()
 
             sized(part, act)
@@ -363,7 +433,7 @@
     sized(blk, waits_keep)
 
     chunks = sub_count * groups
-    near_lag, pair_lag = 2, 4
+    near_lag, pair_lag = 3, 5
 
     def place_of(chunk):
         later = chunk - groups
@@ -377,6 +447,8 @@
         @pl.when((chunk >= groups) & (chunk < chunks))
         def _():
             relay(*place_of(chunk))
+            if chips == 2:
+                forward(*place_of(chunk))
 
         @pl.when(chunk >= pair_lag)
         def _():
@@ -392,11 +464,28 @@
             def _():
                 far(step, group, size).wait_send()
 
-            for hop in range(1, chips):
-                near(hop, step, group, blk, size).wait_send()
+            if chips == 2 and size == heavy:
+
+                @pl.when(step > 0)
+                def _():
+                    early(step, group).wait_send()
+
+                @pl.when(step == 0)
+                def _():
+                    near(1, step, group, blk, size).wait_send()
+
+            else:
+                for hop in range(1, chips):
+                    near(hop, step, group, blk, size).wait_send()
             pair(0, step, group, blk, size).wait_send()
 
         sized(blk, own_act)
+        if chips == 2:
+
+            @pl.when(forwards & (step > 0))
+            def _():
+                far2(step, group).wait_send()
+
         for hop in range(1, chips):
             part = held(hop, core)
             sized(part, lambda size: pair(hop, step, group, part, size).wait_send())
@@ -420,18 +509,36 @@
     source_of[...] = found
 
 
-def phases(source_of, octants, waves, quarters, phase_cos, phase_sin, out):
-    step = pl.program_id(0)
-    count, cases, places, _, _ = out.shape
-    for box in range(count):
-        at = step * count + box
-        source = source_of[at]
-        for place in range(places):
-            octant = octants[place, at]
-            turn_cos = phase_cos[0, octant]
-            turn_sin = phase_sin[0, octant]
-            for case in range(cases):
-                out[box, case, place] = waves[source, case] * turn_cos + quarters[source, case] * turn_sin
+def phases(source_of, octants, waves, quarters, phase_cos, phase_sin, out, blocks, sems):
+    slots, count, cases, places, _, _ = blocks.shape
+    boxes = out.shape[0]
+
+    def send(step):
+        slot = step % slots
+        return pltpu.make_async_copy(blocks.at[slot], out.at[pl.ds(step * count, count)], sems.at[slot])
+
+    @pl.loop(0, boxes // count)
+    def _(step):
+        slot = step % slots
+
+        @pl.when(step >= slots)
+        def _():
+            send(step - slots).wait()
+
+        for box in range(count):
+            at = step * count + box
+            source = source_of[at]
+            for place in range(places):
+                octant = octants[place, at]
+                turn_cos = phase_cos[0, octant]
+                turn_sin = phase_sin[0, octant]
+                for case in range(cases):
+                    blocks[slot, box, case, place] = waves[source, case] * turn_cos + quarters[source, case] * turn_sin
+        send(step).start()
+
+    @pl.loop(boxes // count - slots, boxes // count)
+    def _(step):
+        send(step).wait()
 
 
 def body(coefficients, owner_slot, child_list):
@@ -449,31 +556,33 @@
     rows = max(packed_rows(depth, part) for part in range(parts))
     total_rows = sum(packed_rows(depth, part) for part in range(parts))
     vmem = pl.BlockSpec(memory_space=pltpu.VMEM)
+    dma = pltpu.SemaphoreType.DMA
     at_once = 8
     outgoing, slots = pl.pallas_call(
         pack,
         grid_spec=pltpu.PrefetchScalarGridSpec(
             num_scalar_prefetch=1,
-            grid=(boxes // at_once,),
-            in_specs=[pl.BlockSpec((at_once, lines * depth, columns), lambda i, slot: (i, 0, 0))],
+            grid=(1,),
+            in_specs=[pl.BlockSpec(memory_space=pltpu.HBM)],
             out_specs=(vmem, vmem),
             scratch_shapes=[
                 pltpu.VMEM((rows + 1, at_once, lines, columns), jnp.float32),
                 pltpu.SMEM((sub_count,), jnp.int32),
+                pltpu.VMEM((boxes // at_once, at_once, lines * depth, columns), jnp.float32),
+                dma((boxes // at_once,)),
             ],
         ),
         out_shape=(
             jax.ShapeDtypeStruct((sub_count, groups, rows, each, lines, columns), jnp.float32),
             jax.ShapeDtypeStruct((sub_count, 1, LANES), jnp.int32),
         ),
-        compiler_params=pltpu.CompilerParams(vmem_limit_bytes=12 * MIB),
+        compiler_params=pltpu.CompilerParams(vmem_limit_bytes=16 * MIB),
         name="pack",
     )(owner_slot, coefficients.reshape(boxes, lines * depth, columns))
 
     matrix = wave_matrix(degrees, columns, K)
     high = matrix.astype(jnp.bfloat16)
     low = (matrix - high.astype(np.float32)).astype(jnp.bfloat16)
-    dma = pltpu.SemaphoreType.DMA
     waves, quarters, source_of = pl.pallas_call(
         exchange,
         out_shape=(
@@ -497,6 +606,11 @@
             dma((sub_count,)),
             dma((sub_count,)),
             dma((groups + 1,)),
+            pltpu.VMEM((sub_count, groups, rows, each, lines, columns) if chips == 2 else (8, LANES), jnp.float32),
+            dma((sub_count, groups)),
+            dma((sub_count, groups)),
+            dma((sub_count, groups)),
+            dma((sub_count, groups)),
         ],
         compiler_params=pltpu.CompilerParams(
             collective_id=0, has_side_effects=True, vmem_limit_bytes=40 * MIB
@@ -512,17 +626,20 @@
 
     phase_cos, phase_sin = phase_tables(parts, K)
     blk = lax.axis_index("blk").astype(jnp.int32)
-    count = 2
+    count = 2 if boxes % 2 == 0 else 1
+    slots = min(6, boxes // count)
     own = pl.BlockSpec((1, 8, 2 * width, K), lambda i, source, octants, part: (part[0], 0, 0, 0))
     out = pl.pallas_call(
         lambda source, octants, part, *refs: phases(source, octants, *refs),
         grid_spec=pltpu.PrefetchScalarGridSpec(
             num_scalar_prefetch=3,
-            grid=(boxes // count,),
+            grid=(1,),
             in_specs=[vmem, vmem, own, own],
-            out_specs=pl.BlockSpec(
-                (count, cases, 8, 2 * width, K), lambda i, source, octants, part: (i, 0, 0, 0, 0)
-            ),
+            out_specs=pl.BlockSpec(memory_space=pltpu.HBM),
+            scratch_shapes=[
+                pltpu.VMEM((slots, count, cases, 8, 2 * width, K), jnp.float32),
+                dma((slots,)),
+            ],
         ),
         out_shape=jax.ShapeDtypeStruct((boxes, cases, 8, 2 * width, K), jnp.float32),
         compiler_params=pltpu.CompilerParams(vmem_limit_bytes=32 * MIB),

time: 128 us -> 110 us (0.86)
  the two profiles are of different devices: /device:TPU:9 before, /device:TPU:0 now
where the time goes in v2:
time: 110 us; the launch traced here: 109 us
  Pallas kernels  106 us (96%)
  local copies, waits for them, and re-layouts  2.92 us (3%)
    pallas_call x1, Pallas kernels, body(): pl.pallas_call(exchange, out_shape=(jax.ShapeDtypeStruct((sub_count, grou...  90.7 us
    pallas_call x1, Pallas kernels, body(): pl.pallas_call(lambda source, octants, part, *refs: phases(source, octant...  11.6 us
    pallas_call x1, Pallas kernels, body(): pl.pallas_call(pack, grid_spec=pltpu.PrefetchScalarGridSpec(num_scalar_pr...  3.8 us
    unnamed x24, local copies, waits for them, and re-layouts  2.92 us

profile of v2, /device:TPU:0, one launch (start us, length us, event | category | flops | bytes accessed | tf_op | source)
XLA Modules:
  0.0 109.2 jit_solution(16030417752487832311)
XLA Ops:
  0.0 0.0 copy-start.11
  0.0 0.0 copy-start.9
  0.0 0.0 copy-start
  0.0 2.2 %copy-done = f32[64,4,2,16,128]{4,3,2,1,0:T(8,128)S(1)} copy-done((f32[64,4,2,16,128]{4,3,2,1,0:T(8,128)S(1)}, f32[64,4,2,16,128]{4,3,2,1,0:T(8,128)}, u32[]{:S(2)}) %copy-start) | copy-done | bytes 4194328
  2.2 0.0 copy-start.10
  2.2 0.7 copy-done.10
  2.9 0.0 copy-start.3
  2.9 0.0 copy-start.4
  2.9 0.0 copy-start.5
  2.9 0.0 copy-start.6
  2.9 0.0 copy-start.7
  2.9 0.0 copy-start.8
  2.9 0.0 copy-start.1
  2.9 0.0 copy-start.2
  2.9 3.8 %pack.1 = (f32[8,4,14,2,8,128]{5,4,3,2,1,0:T(8,128)S(1)}, s32[8,1,128]{2,1,0:T(1,128)S(1)}) custom-call(s32[64]{0:T(128)S(1)} %copy-done.10, f32[64,128,128]{2,1,0:T(8,128)S(1)} %bitcast.9), custom_call_target="tpu_custom_call" | custom-call | tf_op jit(solution)/shard_map/pack/pallas_call | solution.py:561
  6.7 0.0 copy-done.11
  6.8 0.0 copy-done.3
  6.8 0.0 copy-done.4
  6.8 0.0 copy-done.5
  6.8 0.0 copy-done.6
  6.8 0.0 copy-done.7
  6.8 0.0 copy-done.8
  6.8 90.7 %exchange.1 = (f32[8,4,2,4,32,128]{5,4,3,2,1,0:T(8,128)S(1)}, f32[8,4,2,4,32,128]{5,4,3,2,1,0:T(8,128)S(1)}, s32[1,128]{1,0:T(1,128)S(1)}) custom-call(f32[8,4,14,2,8,128]{5,4,3,2,1,0:T(8,128)S(1)} %get-tuple-element.10.blocks, s32[8,1,128]{2,1,0:T(1,128)S(1)} %get-tuple-element.11.slots, f32[4,16,128]{2,1,0:T(8,128)S(1)} %copy-done.8, ...), custom_call_target="tpu_custom_call" | custom-call | tf_op jit(solution)/shard_map/exchange/pallas_call | solution.py:586
  97.5 0.0 copy-done.9
  97.5 0.0 copy-done.1
  97.6 0.0 copy-done.2
  97.6 11.6 %phases.1 = f32[64,4,8,32,128]{4,3,2,1,0:T(8,128)} custom-call(s32[128]{0:T(128)S(1)} %bitcast.11, s32[8,64]{1,0:T(8,128)S(1)} %bitcast.10, s32[1]{0:T(128)} %bitcast.3.part, f32[64,4,32,128]{3,2,1,0:T(8,128)S(1)} %bitcast.7, f32[64,4,32,128]{3,2,1,0:T(8,128)S(1)} %bitcast.8, f32[4,8,32,128]{3,2,1,0:T(8,128)S(1)} %copy-done.2, f32[4,8,32,128]{3,2,1,0:T(8,128)S(1)} %copy-done.1), custom_call_target="tpu_custom_call" | custom-call | tf_op jit(solution)/shard_map/phases/pallas_call | solution.py:632
Async XLA Ops:
  0.0 6.8 %copy-start.11 = (f32[1,128]{1,0:T(1,128)S(1)}, f32[1,128]{1,0:T(1,128)}, u32[]{:S(2)}) copy-start(f32[1,128]{1,0:T(1,128)} %constant.24.clone.orders) | copy-start | bytes 1540
  0.0 97.5 %copy-start.9 = (s32[64,8]{0,1:T(8,128)S(1)}, s32[64,8]{0,1:T(8,128)}, u32[]{:S(2)}) copy-start(s32[64,8]{0,1:T(8,128)} %param.14) | copy-start | bytes 6148
  0.0 2.2 %copy-start = (f32[64,4,2,16,128]{4,3,2,1,0:T(8,128)S(1)}, f32[64,4,2,16,128]{4,3,2,1,0:T(8,128)}, u32[]{:S(2)}) copy-start(f32[64,4,2,16,128]{4,3,2,1,0:T(8,128)} %param.12) | copy-start | bytes 12582916
  2.2 0.7 copy-start.10
  2.9 3.9 %copy-start.3 = (bf16[256,256]{1,0:T(8,128)(2,1)S(1)}, bf16[256,256]{1,0:T(8,128)(2,1)}, u32[]{:S(2)}) copy-start(bf16[256,256]{1,0:T(8,128)(2,1)} %constant.28.clone.low) | copy-start | bytes 393220
  2.9 3.9 %copy-start.4 = (bf16[256,256]{1,0:T(8,128)(2,1)S(1)}, bf16[256,256]{1,0:T(8,128)(2,1)}, u32[]{:S(2)}) copy-start(bf16[256,256]{1,0:T(8,128)(2,1)} %constant.27.clone.high) | copy-start | bytes 393220
  2.9 3.9 %copy-start.5 = (f32[64,1,128]{2,1,0:T(1,128)S(1)}, f32[64,1,128]{2,1,0:T(1,128)}, u32[]{:S(2)}) copy-start(f32[64,1,128]{2,1,0:T(1,128)} %constant.26.clone.before) | copy-start | bytes 98308
  2.9 3.9 %copy-start.6 = (f32[64,1,128]{2,1,0:T(1,128)S(1)}, f32[64,1,128]{2,1,0:T(1,128)}, u32[]{:S(2)}) copy-start(f32[64,1,128]{2,1,0:T(1,128)} %constant.25.clone.factor) | copy-start | bytes 98308
  2.9 3.9 %copy-start.7 = (f32[4,16,128]{2,1,0:T(8,128)S(1)}, f32[4,16,128]{2,1,0:T(8,128)}, u32[]{:S(2)}) copy-start(f32[4,16,128]{2,1,0:T(8,128)} %constant.23.clone.cosines) | copy-start | bytes 98308
  2.9 3.9 %copy-start.8 = (f32[4,16,128]{2,1,0:T(8,128)S(1)}, f32[4,16,128]{2,1,0:T(8,128)}, u32[]{:S(2)}) copy-start(f32[4,16,128]{2,1,0:T(8,128)} %constant.22.clone.diag) | copy-start | bytes 98308
  2.9 94.6 %copy-start.1 = (f32[4,8,32,128]{3,2,1,0:T(8,128)S(1)}, f32[4,8,32,128]{3,2,1,0:T(8,128)}, u32[]{:S(2)}) copy-start(f32[4,8,32,128]{3,2,1,0:T(8,128)} %constant.30.clone.refs_3_) | copy-start | bytes 1572868
  2.9 94.6 %copy-start.2 = (f32[4,8,32,128]{3,2,1,0:T(8,128)S(1)}, f32[4,8,32,128]{3,2,1,0:T(8,128)}, u32[]{:S(2)}) copy-start(f32[4,8,32,128]{3,2,1,0:T(8,128)} %constant.29.clone.refs_2_) | copy-start | bytes 1572868

commit v3 on v2

--- a/solution.py
+++ b/solution.py
@@ -185,6 +185,8 @@
     recv_early,
     send_far2,
     recv_far2,
+    send_back,
+    recv_back,
 ):
     sub_count, groups, _, each, lines, columns = blocks.shape
     degrees, width, _, _ = tab.shape
@@ -292,6 +294,23 @@
             local.at[group],
         )
 
+    def lean(group):
+        return group % 2 == 0
+
+    def direct(group, size):
+        return jnp.logical_not(lean(group)) if chips == 2 and size == heavy else group >= 0
+
+    def back(step, group):
+        source = swapped(sub, step, sub_count)
+        rows = pl.ds(heavy_rows, heavy)
+        return remote(
+            gathered.at[source, group, rows],
+            gathered.at[source, group, rows],
+            send_back.at[step, group],
+            recv_back.at[step, group],
+            (sub, parts - 1),
+        )
+
     barrier = pltpu.get_barrier_semaphore()
 
     def greet(device):
@@ -305,7 +324,6 @@
     pl.semaphore_wait(barrier, sub_count - 1 + chips)
 
     others = sub_count - 1
-    ahead = 1
 
     def step_at(index):
         return 1 + (index + sub_count // 2 - 1) % others
@@ -316,11 +334,13 @@
     keep_slot.start()
 
     def begin(size):
-        @pl.loop(0, min(ahead, groups))
+        @pl.loop(0, groups)
         def _(group):
-            @pl.loop(0, others)
-            def _(index):
-                far(step_at(index), group, size).start()
+            @pl.when(direct(group, size))
+            def _():
+                @pl.loop(0, others)
+                def _(index):
+                    far(step_at(index), group, size).start()
 
         @pl.loop(0, groups)
         def _(group):
@@ -347,17 +367,15 @@
 
     def relay(step, group):
         def act(size):
-            far(step, group, size).wait_recv()
-            if chips != 2:
-                for hop in range(1, chips):
-                    near(hop, step, group, blk, size).start()
-            elif size != heavy:
-                near(1, step, group, blk, size).start()
-            pair(0, step, group, blk, size).start()
-
-            @pl.when(group + ahead < groups)
+            @pl.when(direct(group, size))
             def _():
-                far(step, group + ahead, size).start()
+                far(step, group, size).wait_recv()
+                if chips != 2:
+                    for hop in range(1, chips):
+                        near(hop, step, group, blk, size).start()
+                elif size != heavy:
+                    near(1, step, group, blk, size).start()
+                pair(0, step, group, blk, size).start()
 
         sized(blk, act)
 
@@ -378,6 +396,10 @@
                     def _():
                         far2(step, group).wait_recv()
 
+                        @pl.when(lean(group))
+                        def _():
+                            back(step, group).start()
+
                     @pl.when(step == 0)
                     def _():
                         near(hop, step, group, part, size).wait_recv()
@@ -387,6 +409,12 @@
                 pair(hop, step, group, part, size).start()
 
             sized(part, act)
+        if chips == 2:
+
+            @pl.when(feeds & (step > 0) & lean(group))
+            def _():
+                back(step, group).wait_recv()
+                pair(0, step, group, blk, heavy).start()
 
     def finish(step, group):
         for hop in range(chips):
@@ -460,7 +488,7 @@
 
     def drain(step, group):
         def own_act(size):
-            @pl.when(step > 0)
+            @pl.when((step > 0) & direct(group, size))
             def _():
                 far(step, group, size).wait_send()
 
@@ -485,6 +513,10 @@
             @pl.when(forwards & (step > 0))
             def _():
                 far2(step, group).wait_send()
+
+                @pl.when(lean(group))
+                def _():
+                    back(step, group).wait_send()
 
         for hop in range(1, chips):
             part = held(hop, core)
@@ -576,7 +608,7 @@
             jax.ShapeDtypeStruct((sub_count, groups, rows, each, lines, columns), jnp.float32),
             jax.ShapeDtypeStruct((sub_count, 1, LANES), jnp.int32),
         ),
-        compiler_params=pltpu.CompilerParams(vmem_limit_bytes=16 * MIB),
+        compiler_params=pltpu.CompilerParams(vmem_limit_bytes=48 * MIB),
         name="pack",
     )(owner_slot, coefficients.reshape(boxes, lines * depth, columns))
 
@@ -611,6 +643,8 @@
             dma((sub_count, groups)),
             dma((sub_count, groups)),
             dma((sub_count, groups)),
+            dma((sub_count, groups)),
+            dma((sub_count, groups)),
         ],
         compiler_params=pltpu.CompilerParams(
             collective_id=0, has_side_effects=True, vmem_limit_bytes=40 * MIB

time: 110 us -> 106 us (0.964)
  local copies, waits for them, and re-layouts: 2.92 us -> 0.79 us
    unnamed x24 -> x22, local copies, waits for them, and re-layouts: 2.92 us -> 0.79 us
    pallas_call x1, Pallas kernels: 90.7 us -> 88.9 us  [body(): pl.pallas_call(exchange, out_shape=(jax.ShapeDtypeStruct((sub_count, grou...]
where the time goes in v3:
time: 106 us
  Pallas kernels  105 us (99%)
    pallas_call x1, Pallas kernels, body(): pl.pallas_call(exchange, out_shape=(jax.ShapeDtypeStruct((sub_count, grou...  88.9 us
    pallas_call x1, Pallas kernels, body(): pl.pallas_call(lambda source, octants, part, *refs: phases(source, octant...  11.7 us
    pallas_call x1, Pallas kernels, body(): pl.pallas_call(pack, grid_spec=pltpu.PrefetchScalarGridSpec(num_scalar_pr...  4.51 us

profile of v3, /device:TPU:0, one launch (start us, length us, event | category | flops | bytes accessed | tf_op | source)
XLA Modules:
  0.0 106.0 jit_solution(17450087074168091032)
XLA Ops:
  0.0 0.0 copy-start.2
  0.0 0.0 copy-start.3
  0.0 0.0 copy-start.4
  0.0 0.0 copy-start.5
  0.0 0.0 copy-start.6
  0.0 0.0 copy-start.7
  0.0 0.0 copy-start
  0.0 0.0 copy-start.1
  0.1 0.0 copy-start.8
  0.1 0.0 copy-start.9
  0.1 0.7 copy-done.9
  0.8 0.0 copy-start.10
  0.8 4.5 %pack.1 = (f32[8,4,14,2,8,128]{5,4,3,2,1,0:T(8,128)S(1)}, s32[8,1,128]{2,1,0:T(1,128)S(1)}) custom-call(s32[64]{0:T(128)S(1)} %copy-done.9, f32[64,128,128]{2,1,0:T(8,128)} %bitcast.11), custom_call_target="tpu_custom_call" | custom-call | tf_op jit(solution)/shard_map/pack/pallas_call | solution.py:593
  5.3 0.0 copy-done.2
  5.4 0.0 copy-done.3
  5.4 0.0 copy-done.4
  5.4 0.0 copy-done.5
  5.4 0.0 copy-done.6
  5.4 0.0 copy-done.7
  5.4 0.0 copy-done.10
  5.4 88.9 %exchange.1 = (f32[8,4,2,4,32,128]{5,4,3,2,1,0:T(8,128)S(1)}, f32[8,4,2,4,32,128]{5,4,3,2,1,0:T(8,128)S(1)}, s32[1,128]{1,0:T(1,128)S(1)}) custom-call(f32[8,4,14,2,8,128]{5,4,3,2,1,0:T(8,128)S(1)} %get-tuple-element.10.blocks, s32[8,1,128]{2,1,0:T(1,128)S(1)} %get-tuple-element.11.slots, f32[4,16,128]{2,1,0:T(8,128)S(1)} %copy-done.7, ...), custom_call_target="tpu_custom_call" | custom-call | tf_op jit(solution)/shard_map/exchange/pallas_call | solution.py:618
  94.3 0.0 copy-done
  94.3 0.0 copy-done.1
  94.4 0.0 copy-done.8
  94.4 11.7 %phases.1 = f32[64,4,8,32,128]{4,3,2,1,0:T(8,128)} custom-call(s32[128]{0:T(128)S(1)} %bitcast.10, s32[8,64]{1,0:T(8,128)S(1)} %bitcast.9, s32[1]{0:T(128)} %bitcast.3.part, f32[64,4,32,128]{3,2,1,0:T(8,128)S(1)} %bitcast.7, f32[64,4,32,128]{3,2,1,0:T(8,128)S(1)} %bitcast.8, f32[4,8,32,128]{3,2,1,0:T(8,128)S(1)} %copy-done.1, f32[4,8,32,128]{3,2,1,0:T(8,128)S(1)} %copy-done), custom_call_target="tpu_custom_call" | custom-call | tf_op jit(solution)/shard_map/phases/pallas_call | solution.py:666
Async XLA Ops:
  0.0 5.3 %copy-start.2 = (bf16[256,256]{1,0:T(8,128)(2,1)S(1)}, bf16[256,256]{1,0:T(8,128)(2,1)}, u32[]{:S(2)}) copy-start(bf16[256,256]{1,0:T(8,128)(2,1)} %constant.28.clone.low) | copy-start | bytes 393220
  0.0 5.4 %copy-start.3 = (bf16[256,256]{1,0:T(8,128)(2,1)S(1)}, bf16[256,256]{1,0:T(8,128)(2,1)}, u32[]{:S(2)}) copy-start(bf16[256,256]{1,0:T(8,128)(2,1)} %constant.27.clone.high) | copy-start | bytes 393220
  0.0 5.4 %copy-start.4 = (f32[64,1,128]{2,1,0:T(1,128)S(1)}, f32[64,1,128]{2,1,0:T(1,128)}, u32[]{:S(2)}) copy-start(f32[64,1,128]{2,1,0:T(1,128)} %constant.26.clone.before) | copy-start | bytes 98308
  0.0 5.4 %copy-start.5 = (f32[64,1,128]{2,1,0:T(1,128)S(1)}, f32[64,1,128]{2,1,0:T(1,128)}, u32[]{:S(2)}) copy-start(f32[64,1,128]{2,1,0:T(1,128)} %constant.25.clone.factor) | copy-start | bytes 98308
  0.0 5.4 %copy-start.6 = (f32[4,16,128]{2,1,0:T(8,128)S(1)}, f32[4,16,128]{2,1,0:T(8,128)}, u32[]{:S(2)}) copy-start(f32[4,16,128]{2,1,0:T(8,128)} %constant.23.clone.cosines) | copy-start | bytes 98308
  0.0 5.4 %copy-start.7 = (f32[4,16,128]{2,1,0:T(8,128)S(1)}, f32[4,16,128]{2,1,0:T(8,128)}, u32[]{:S(2)}) copy-start(f32[4,16,128]{2,1,0:T(8,128)} %constant.22.clone.diag) | copy-start | bytes 98308
  0.0 94.3 %copy-start = (f32[4,8,32,128]{3,2,1,0:T(8,128)S(1)}, f32[4,8,32,128]{3,2,1,0:T(8,128)}, u32[]{:S(2)}) copy-start(f32[4,8,32,128]{3,2,1,0:T(8,128)} %constant.30.clone.refs_3_) | copy-start | bytes 1572868
  0.0 94.3 %copy-start.1 = (f32[4,8,32,128]{3,2,1,0:T(8,128)S(1)}, f32[4,8,32,128]{3,2,1,0:T(8,128)}, u32[]{:S(2)}) copy-start(f32[4,8,32,128]{3,2,1,0:T(8,128)} %constant.29.clone.refs_2_) | copy-start | bytes 1572868
  0.1 94.3 %copy-start.8 = (s32[64,8]{0,1:T(8,128)S(1)}, s32[64,8]{0,1:T(8,128)}, u32[]{:S(2)}) copy-start(s32[64,8]{0,1:T(8,128)} %param.14) | copy-start | bytes 6148
  0.1 0.8 copy-start.9
  0.8 4.6 %copy-start.10 = (f32[1,128]{1,0:T(1,128)S(1)}, f32[1,128]{1,0:T(1,128)}, u32[]{:S(2)}) copy-start(f32[1,128]{1,0:T(1,128)} %constant.24.clone.orders) | copy-start | bytes 1540

commit v4 on v3

--- a/solution.py
+++ b/solution.py
@@ -93,7 +93,7 @@
     return per_part(np.cos(phase)), per_part(np.sin(phase))
 
 
-def pack(slot, source, out, placed, stage, count, arrived, sems):
+def pack(slots, source, out, placed, stage, count, slot, arrived, sems):
     blk = lax.axis_index("blk")
     _, at_once, depth_lines, columns = arrived.shape
     sub_count, groups, rows, each, lines, _ = out.shape
@@ -104,6 +104,8 @@
     def fetch(step):
         return pltpu.make_async_copy(source.at[pl.ds(step * at_once, at_once)], arrived.at[step], sems.at[step])
 
+    fetch_slot = pltpu.make_async_copy(slots, slot, sems.at[steps])
+    fetch_slot.start()
     for step in range(steps):
         fetch(step).start()
     stage[...] = jnp.zeros_like(stage)
@@ -112,6 +114,7 @@
         count[sub] = 0
     lane = lax.broadcasted_iota(jnp.int32, (at_once, lines, columns), 2)
     slot_lane = lax.broadcasted_iota(jnp.int32, (1, LANES), 1)
+    fetch_slot.wait()
 
     @pl.loop(0, steps)
     def _(step):
@@ -461,7 +464,7 @@
     sized(blk, waits_keep)
 
     chunks = sub_count * groups
-    near_lag, pair_lag = 3, 5
+    near_lag, pair_lag = 5, 7
 
     def place_of(chunk):
         later = chunk - groups
@@ -592,18 +595,15 @@
     at_once = 8
     outgoing, slots = pl.pallas_call(
         pack,
-        grid_spec=pltpu.PrefetchScalarGridSpec(
-            num_scalar_prefetch=1,
-            grid=(1,),
-            in_specs=[pl.BlockSpec(memory_space=pltpu.HBM)],
-            out_specs=(vmem, vmem),
-            scratch_shapes=[
-                pltpu.VMEM((rows + 1, at_once, lines, columns), jnp.float32),
-                pltpu.SMEM((sub_count,), jnp.int32),
-                pltpu.VMEM((boxes // at_once, at_once, lines * depth, columns), jnp.float32),
-                dma((boxes // at_once,)),
-            ],
-        ),
+        in_specs=[pl.BlockSpec(memory_space=pltpu.HBM)] * 2,
+        out_specs=(vmem, vmem),
+        scratch_shapes=[
+            pltpu.VMEM((rows + 1, at_once, lines, columns), jnp.float32),
+            pltpu.SMEM((sub_count,), jnp.int32),
+            pltpu.SMEM((boxes,), jnp.int32),
+            pltpu.VMEM((boxes // at_once, at_once, lines * depth, columns), jnp.float32),
+            dma((boxes // at_once + 1,)),
+        ],
         out_shape=(
             jax.ShapeDtypeStruct((sub_count, groups, rows, each, lines, columns), jnp.float32),
             jax.ShapeDtypeStruct((sub_count, 1, LANES), jnp.int32),

time: 106 us -> 103 us (0.972)
  Pallas kernels: 105 us -> 102 us
    pallas_call x1, Pallas kernels: 88.9 us -> 85.9 us  [body(): pl.pallas_call(exchange, out_shape=(jax.ShapeDtypeStruct((sub_count, grou...]
where the time goes in v4:
time: 103 us
  Pallas kernels  102 us (99%)
    pallas_call x1, Pallas kernels, body(): pl.pallas_call(exchange, out_shape=(jax.ShapeDtypeStruct((sub_count, grou...  85.9 us
    pallas_call x1, Pallas kernels, body(): pl.pallas_call(lambda source, octants, part, *refs: phases(source, octant...  11.7 us
    pallas_call x1, Pallas kernels, body(): pl.pallas_call(pack, in_specs=[pl.BlockSpec(memory_space=pltpu.HBM)] * 2,...  3.99 us

profile of v4, /device:TPU:0, one launch (start us, length us, event | category | flops | bytes accessed | tf_op | source)
XLA Modules:
  0.0 102.5 jit_solution(15349481105331680758)
XLA Ops:
  0.0 0.0 copy-start.2
  0.0 0.0 copy-start.3
  0.0 0.0 copy-start.4
  0.0 0.0 copy-start.5
  0.0 0.0 copy-start.6
  0.0 0.0 copy-start.7
  0.0 0.0 copy-start
  0.0 0.0 copy-start.1
  0.1 0.0 copy-start.8
  0.1 0.0 copy-start.9
  0.1 0.7 copy-done.9
  0.8 0.0 copy-start.10
  0.8 4.0 %pack.1 = (f32[8,4,14,2,8,128]{5,4,3,2,1,0:T(8,128)S(1)}, s32[8,1,128]{2,1,0:T(1,128)S(1)}) custom-call(s32[64]{0:T(128)S(1)} %copy-done.9, f32[64,128,128]{2,1,0:T(8,128)} %bitcast.11), custom_call_target="tpu_custom_call" | custom-call | tf_op jit(solution)/shard_map/pack/pallas_call | solution.py:596
  4.8 0.0 copy-done.2
  4.8 0.0 copy-done.3
  4.8 0.0 copy-done.4
  4.9 0.0 copy-done.5
  4.9 0.0 copy-done.6
  4.9 0.0 copy-done.7
  4.9 0.0 copy-done.10
  4.9 85.9 %exchange.1 = (f32[8,4,2,4,32,128]{5,4,3,2,1,0:T(8,128)S(1)}, f32[8,4,2,4,32,128]{5,4,3,2,1,0:T(8,128)S(1)}, s32[1,128]{1,0:T(1,128)S(1)}) custom-call(f32[8,4,14,2,8,128]{5,4,3,2,1,0:T(8,128)S(1)} %get-tuple-element.10.blocks, s32[8,1,128]{2,1,0:T(1,128)S(1)} %get-tuple-element.11.slots, f32[4,16,128]{2,1,0:T(8,128)S(1)} %copy-done.7, ...), custom_call_target="tpu_custom_call" | custom-call | tf_op jit(solution)/shard_map/exchange/pallas_call | solution.py:618
  90.8 0.0 copy-done
  90.9 0.0 copy-done.1
  90.9 0.0 copy-done.8
  90.9 11.7 %phases.1 = f32[64,4,8,32,128]{4,3,2,1,0:T(8,128)} custom-call(s32[128]{0:T(128)S(1)} %bitcast.10, s32[8,64]{1,0:T(8,128)S(1)} %bitcast.9, s32[1]{0:T(128)} %bitcast.3.part, f32[64,4,32,128]{3,2,1,0:T(8,128)S(1)} %bitcast.7, f32[64,4,32,128]{3,2,1,0:T(8,128)S(1)} %bitcast.8, f32[4,8,32,128]{3,2,1,0:T(8,128)S(1)} %copy-done.1, f32[4,8,32,128]{3,2,1,0:T(8,128)S(1)} %copy-done), custom_call_target="tpu_custom_call" | custom-call | tf_op jit(solution)/shard_map/phases/pallas_call | solution.py:666
Async XLA Ops:
  0.0 4.8 %copy-start.2 = (bf16[256,256]{1,0:T(8,128)(2,1)S(1)}, bf16[256,256]{1,0:T(8,128)(2,1)}, u32[]{:S(2)}) copy-start(bf16[256,256]{1,0:T(8,128)(2,1)} %constant.28.clone.low) | copy-start | bytes 393220
  0.0 4.8 %copy-start.3 = (bf16[256,256]{1,0:T(8,128)(2,1)S(1)}, bf16[256,256]{1,0:T(8,128)(2,1)}, u32[]{:S(2)}) copy-start(bf16[256,256]{1,0:T(8,128)(2,1)} %constant.27.clone.high) | copy-start | bytes 393220
  0.0 4.8 %copy-start.4 = (f32[64,1,128]{2,1,0:T(1,128)S(1)}, f32[64,1,128]{2,1,0:T(1,128)}, u32[]{:S(2)}) copy-start(f32[64,1,128]{2,1,0:T(1,128)} %constant.26.clone.before) | copy-start | bytes 98308
  0.0 4.8 %copy-start.5 = (f32[64,1,128]{2,1,0:T(1,128)S(1)}, f32[64,1,128]{2,1,0:T(1,128)}, u32[]{:S(2)}) copy-start(f32[64,1,128]{2,1,0:T(1,128)} %constant.25.clone.factor) | copy-start | bytes 98308
  0.0 4.9 %copy-start.6 = (f32[4,16,128]{2,1,0:T(8,128)S(1)}, f32[4,16,128]{2,1,0:T(8,128)}, u32[]{:S(2)}) copy-start(f32[4,16,128]{2,1,0:T(8,128)} %constant.23.clone.cosines) | copy-start | bytes 98308
  0.0 4.9 %copy-start.7 = (f32[4,16,128]{2,1,0:T(8,128)S(1)}, f32[4,16,128]{2,1,0:T(8,128)}, u32[]{:S(2)}) copy-start(f32[4,16,128]{2,1,0:T(8,128)} %constant.22.clone.diag) | copy-start | bytes 98308
  0.0 90.8 %copy-start = (f32[4,8,32,128]{3,2,1,0:T(8,128)S(1)}, f32[4,8,32,128]{3,2,1,0:T(8,128)}, u32[]{:S(2)}) copy-start(f32[4,8,32,128]{3,2,1,0:T(8,128)} %constant.30.clone.refs_3_) | copy-start | bytes 1572868
  0.0 90.8 %copy-start.1 = (f32[4,8,32,128]{3,2,1,0:T(8,128)S(1)}, f32[4,8,32,128]{3,2,1,0:T(8,128)}, u32[]{:S(2)}) copy-start(f32[4,8,32,128]{3,2,1,0:T(8,128)} %constant.29.clone.refs_2_) | copy-start | bytes 1572868
  0.1 90.8 %copy-start.8 = (s32[64,8]{0,1:T(8,128)S(1)}, s32[64,8]{0,1:T(8,128)}, u32[]{:S(2)}) copy-start(s32[64,8]{0,1:T(8,128)} %param.14) | copy-start | bytes 6148
  0.1 0.8 copy-start.9
  0.8 4.1 %copy-start.10 = (f32[1,128]{1,0:T(1,128)S(1)}, f32[1,128]{1,0:T(1,128)}, u32[]{:S(2)}) copy-start(f32[1,128]{1,0:T(1,128)} %constant.24.clone.orders) | copy-start | bytes 1540

commit v5 on v4

--- a/solution.py
+++ b/solution.py
@@ -127,8 +127,8 @@
             value = arrived[step, :, pl.ds(inner, lines, depth), :]
             value = pltpu.roll(value, (offset + LANES + degree - columns // 2) % LANES, 2)
             here = (lane >= offset) & (lane < end)
-            stage[row] = jnp.where(here, value, stage[row])
-            stage[row + 1] = jnp.where(lane < end - LANES, value, stage[row + 1])
+            pltpu.store(stage.at[row], value, mask=here)
+            pltpu.store(stage.at[row + 1], value, mask=lane < end - LANES)
         for box in range(at_once):
             own = slot[step * at_once + box]
             target = own // total
@@ -610,7 +610,10 @@
         ),
         compiler_params=pltpu.CompilerParams(vmem_limit_bytes=48 * MIB),
         name="pack",
-    )(owner_slot, coefficients.reshape(boxes, lines * depth, columns))
+    )(
+        pltpu.with_memory_space_constraint(owner_slot, pltpu.HBM),
+        coefficients.reshape(boxes, lines * depth, columns),
+    )
 
     matrix = wave_matrix(degrees, columns, K)
     high = matrix.astype(jnp.bfloat16)

time: 103 us -> 102 us (level)
  no operation moved by 1% of the time
where the time goes in v5:
time: 102 us
  Pallas kernels  102 us (100%)
    pallas_call x1, Pallas kernels, body(): pl.pallas_call(exchange, out_shape=(jax.ShapeDtypeStruct((sub_count, grou...  85.9 us
    pallas_call x1, Pallas kernels, body(): pl.pallas_call(lambda source, octants, part, *refs: phases(source, octant...  11.7 us
    pallas_call x1, Pallas kernels, body(): pl.pallas_call(pack, in_specs=[pl.BlockSpec(memory_space=pltpu.HBM)] * 2,...  3.97 us

profile of v5, /device:TPU:0, one launch (start us, length us, event | category | flops | bytes accessed | tf_op | source)
XLA Modules:
  0.0 101.8 jit_solution(5337024349840205442)
XLA Ops:
  0.0 0.0 copy-start.2
  0.0 0.0 copy-start.3
  0.0 0.0 copy-start.4
  0.0 0.0 copy-start.5
  0.0 0.0 copy-start.9
  0.0 0.0 copy-start.6
  0.0 0.0 copy-start.7
  0.0 0.0 copy-start
  0.1 0.0 copy-start.1
  0.1 0.0 copy-start.8
  0.1 4.0 %pack.1 = (f32[8,4,14,2,8,128]{5,4,3,2,1,0:T(8,128)S(1)}, s32[8,1,128]{2,1,0:T(1,128)S(1)}) custom-call(s32[64]{0:T(128)} %slots.1, f32[64,128,128]{2,1,0:T(8,128)} %bitcast.11), custom_call_target="tpu_custom_call" | custom-call | tf_op jit(solution)/shard_map/pack/pallas_call | solution.py:596
  4.1 0.0 copy-done.2
  4.1 0.0 copy-done.3
  4.1 0.0 copy-done.4
  4.1 0.0 copy-done.5
  4.1 0.0 copy-done.9
  4.1 0.0 copy-done.6
  4.1 0.0 copy-done.7
  4.1 85.9 %exchange.1 = (f32[8,4,2,4,32,128]{5,4,3,2,1,0:T(8,128)S(1)}, f32[8,4,2,4,32,128]{5,4,3,2,1,0:T(8,128)S(1)}, s32[1,128]{1,0:T(1,128)S(1)}) custom-call(f32[8,4,14,2,8,128]{5,4,3,2,1,0:T(8,128)S(1)} %get-tuple-element.10.blocks, s32[8,1,128]{2,1,0:T(1,128)S(1)} %get-tuple-element.11.slots, f32[4,16,128]{2,1,0:T(8,128)S(1)} %copy-done.7, ...), custom_call_target="tpu_custom_call" | custom-call | tf_op jit(solution)/shard_map/exchange/pallas_call | solution.py:621
  90.1 0.0 copy-done
  90.1 0.0 copy-done.1
  90.1 0.0 copy-done.8
  90.1 11.7 %phases.1 = f32[64,4,8,32,128]{4,3,2,1,0:T(8,128)} custom-call(s32[128]{0:T(128)S(1)} %bitcast.10, s32[8,64]{1,0:T(8,128)S(1)} %bitcast.9, s32[1]{0:T(128)} %bitcast.3.part, f32[64,4,32,128]{3,2,1,0:T(8,128)S(1)} %bitcast.7, f32[64,4,32,128]{3,2,1,0:T(8,128)S(1)} %bitcast.8, f32[4,8,32,128]{3,2,1,0:T(8,128)S(1)} %copy-done.1, f32[4,8,32,128]{3,2,1,0:T(8,128)S(1)} %copy-done), custom_call_target="tpu_custom_call" | custom-call | tf_op jit(solution)/shard_map/phases/pallas_call | solution.py:669
Async XLA Ops:
  0.0 4.1 %copy-start.2 = (bf16[256,256]{1,0:T(8,128)(2,1)S(1)}, bf16[256,256]{1,0:T(8,128)(2,1)}, u32[]{:S(2)}) copy-start(bf16[256,256]{1,0:T(8,128)(2,1)} %constant.28.clone.low) | copy-start | bytes 393220
  0.0 4.1 %copy-start.3 = (bf16[256,256]{1,0:T(8,128)(2,1)S(1)}, bf16[256,256]{1,0:T(8,128)(2,1)}, u32[]{:S(2)}) copy-start(bf16[256,256]{1,0:T(8,128)(2,1)} %constant.27.clone.high) | copy-start | bytes 393220
  0.0 4.1 %copy-start.4 = (f32[64,1,128]{2,1,0:T(1,128)S(1)}, f32[64,1,128]{2,1,0:T(1,128)}, u32[]{:S(2)}) copy-start(f32[64,1,128]{2,1,0:T(1,128)} %constant.26.clone.before) | copy-start | bytes 98308
  0.0 4.1 %copy-start.5 = (f32[64,1,128]{2,1,0:T(1,128)S(1)}, f32[64,1,128]{2,1,0:T(1,128)}, u32[]{:S(2)}) copy-start(f32[64,1,128]{2,1,0:T(1,128)} %constant.25.clone.factor) | copy-start | bytes 98308
  0.0 4.1 %copy-start.9 = (f32[1,128]{1,0:T(1,128)S(1)}, f32[1,128]{1,0:T(1,128)}, u32[]{:S(2)}) copy-start(f32[1,128]{1,0:T(1,128)} %constant.24.clone.orders) | copy-start | bytes 1540
  0.0 4.1 %copy-start.6 = (f32[4,16,128]{2,1,0:T(8,128)S(1)}, f32[4,16,128]{2,1,0:T(8,128)}, u32[]{:S(2)}) copy-start(f32[4,16,128]{2,1,0:T(8,128)} %constant.23.clone.cosines) | copy-start | bytes 98308
  0.0 4.1 %copy-start.7 = (f32[4,16,128]{2,1,0:T(8,128)S(1)}, f32[4,16,128]{2,1,0:T(8,128)}, u32[]{:S(2)}) copy-start(f32[4,16,128]{2,1,0:T(8,128)} %constant.22.clone.diag) | copy-start | bytes 98308
  0.0 90.0 %copy-start = (f32[4,8,32,128]{3,2,1,0:T(8,128)S(1)}, f32[4,8,32,128]{3,2,1,0:T(8,128)}, u32[]{:S(2)}) copy-start(f32[4,8,32,128]{3,2,1,0:T(8,128)} %constant.30.clone.refs_3_) | copy-start | bytes 1572868
  0.1 90.0 %copy-start.1 = (f32[4,8,32,128]{3,2,1,0:T(8,128)S(1)}, f32[4,8,32,128]{3,2,1,0:T(8,128)}, u32[]{:S(2)}) copy-start(f32[4,8,32,128]{3,2,1,0:T(8,128)} %constant.29.clone.refs_2_) | copy-start | bytes 1572868
  0.1 90.0 %copy-start.8 = (s32[64,8]{0,1:T(8,128)S(1)}, s32[64,8]{0,1:T(8,128)}, u32[]{:S(2)}) copy-start(s32[64,8]{0,1:T(8,128)} %param.14) | copy-start | bytes 6148
